TPU v7x, 256 devices: a whole 4x4x8 slice. The times are simulated.
256 devices in a mesh: row: 16 (over z_lo, x, core), col: 16 (over y, z_hi).
Axes of the slice: x: 4, y: 4, z: 8 (z_hi: 4, z_lo: 2; z = z_hi * 2 + z_lo), core: 2. Of those that a mesh axis runs over, the one named last changes fastest.
Arguments:
- matrix_tiles: float32 [1, 16, 1, 16, 1024, 1024], P(None, 'row', None, 'col'), may hold values from -17 to 17, as said below
- panels: float32 [3, 1, 16, 512, 128], P(None, None, 'row', 'col'), may hold values from -0.25 to 0.25
- plan: int32 [3, 16], replicated, may hold values 0 or 1
Outputs:
- updated_tiles: float32 [1, 16, 1, 16, 1024, 1024], P(None, 'row', None, 'col')
Inputs may be any that keep to these rules, and one draw needn't show every extreme that they name: `matrix_tiles`: entries below the first subdiagonal of the matrix are zero.
All inputs are finite; a program needn't handle non-finite values.
Results may differ from a plain program's by a relative error of at most 0.0003.
Values sent between devices are 32-bit elements; how exact they have to be, the bound alone decides.
A program may use at most 64 MiB of HBM per device.

v0:
```python
import jax
import jax.numpy as jnp
from jax import lax
from jax.sharding import PartitionSpec as P

exact_mode = lax.Precision.HIGHEST


def broadcast(value, axis, source):
    kept = jnp.where(lax.axis_index(axis) == source, value, 0).astype(value.dtype)
    return lax.psum(kept, axis)


def passed_along(value, axis, steps):
    count = lax.axis_size(axis)
    pairs = [(source, (source + steps) % count) for source in range(count)]
    return lax.ppermute(value, axis, pairs)


def round_offsets(tile_size, window):
    return [0, tile_size - window // 2, window // 2]


def upper_inverse(upper_part):
    order_n = upper_part.shape[0]
    identity = jnp.eye(order_n, dtype=upper_part.dtype)
    scale = 1.0 / jnp.diag(upper_part)
    power = identity - upper_part * scale[:, None]
    result = identity + power
    span = 2
    while span < order_n:
        power = jnp.dot(power, power, precision=exact_mode)
        result = jnp.dot(result, identity + power, precision=exact_mode)
        span = span * 2
    return result * scale[None, :]


def window_factor(reflect):
    window, reflectors = reflect.shape
    gram_matrix = jnp.dot(reflect.T, reflect, precision=exact_mode)
    upper_part = jnp.triu(gram_matrix, 1) + jnp.diag(jnp.diag(gram_matrix) * 0.5)
    factor = upper_inverse(upper_part)
    product = jnp.dot(reflect, factor, precision=exact_mode)
    return jnp.eye(window, dtype=reflect.dtype) - jnp.dot(product, reflect.T, precision=exact_mode)


def live_mask(plan, tile_ids, offsets, window, tile_size):
    chosen = jnp.take(plan, tile_ids, axis=1) > 0
    inside = jnp.stack(
        [
            tile_ids < plan.shape[1] - 1 if offset + window > tile_size else tile_ids >= 0
            for offset in offsets
        ]
    )
    return jnp.logical_and(chosen, inside)


def on_device(matrix_tiles, panels, plan):
    rows_n = lax.axis_size("row")
    cols_n = lax.axis_size("col")
    row_at = lax.axis_index("row")
    col_at = lax.axis_index("col")
    row_tiles, _, col_tiles, _, tile_size, _ = matrix_tiles.shape
    rounds, _, _, _, reflectors = panels.shape
    matrix = matrix_tiles.reshape(row_tiles, col_tiles, tile_size, tile_size)
    gathered = lax.all_gather(panels, "col", axis=3, tiled=True)
    window = gathered.shape[3]
    half_width = window // 2
    panel_all = gathered.reshape(rounds, row_tiles, window, reflectors)
    offsets = round_offsets(tile_size, window)
    identity = jnp.eye(window, dtype=jnp.float32)
    factors = jax.vmap(window_factor)(panel_all.reshape(-1, window, reflectors)).reshape(
        rounds, row_tiles, window, window
    )
    left_ids = jnp.arange(row_tiles, dtype=jnp.int32) * rows_n + row_at
    left_live = live_mask(plan, left_ids, offsets, window, tile_size)
    left_q = jnp.where(left_live[:, :, None, None], factors, identity)
    right_ids = jnp.arange(col_tiles, dtype=jnp.int32) * cols_n + col_at
    source_row = col_at % rows_n
    picked = right_ids // rows_n
    received = broadcast(factors, "row", source_row)
    right_raw = jnp.take(received, picked, axis=1)
    right_live = live_mask(plan, right_ids, offsets, window, tile_size)
    right_q = jnp.where(right_live[:, :, None, None], right_raw, identity)
    last_row = row_at == rows_n - 1
    last_col = col_at == cols_n - 1
    for round_at in range(rounds):
        offset = offsets[round_at]
        left_now = left_q[round_at]
        right_now = right_q[round_at]
        if offset + window <= tile_size:
            window_rows = matrix[:, :, offset : offset + window, :]
            updated = jnp.einsum("ivw,ijvx->ijwx", left_now, window_rows, precision=exact_mode)
            matrix = matrix.at[:, :, offset : offset + window, :].set(updated)
            window_cols = matrix[:, :, :, offset : offset + window]
            updated = jnp.einsum("ijyv,jvw->ijyw", window_cols, right_now, precision=exact_mode)
            matrix = matrix.at[:, :, :, offset : offset + window].set(updated)
        else:
            from_below = passed_along(matrix[:, :, :half_width, :], "row", -1)
            from_below = jnp.where(last_row, jnp.roll(from_below, -1, axis=0), from_below)
            stacked = jnp.concatenate(
                [matrix[:, :, tile_size - half_width :, :], from_below], axis=2
            )
            updated = jnp.einsum("ivw,ijvx->ijwx", left_now, stacked, precision=exact_mode)
            going_back = updated[:, :, half_width:, :]
            going_back = jnp.where(last_row, jnp.roll(going_back, 1, axis=0), going_back)
            returned = passed_along(going_back, "row", 1)
            matrix = matrix.at[:, :, tile_size - half_width :, :].set(updated[:, :, :half_width, :])
            matrix = matrix.at[:, :, :half_width, :].set(returned)
            from_right = passed_along(matrix[:, :, :, :half_width], "col", -1)
            from_right = jnp.where(last_col, jnp.roll(from_right, -1, axis=1), from_right)
            stacked = jnp.concatenate(
                [matrix[:, :, :, tile_size - half_width :], from_right], axis=3
            )
            updated = jnp.einsum("ijyv,jvw->ijyw", stacked, right_now, precision=exact_mode)
            going_back = updated[:, :, :, half_width:]
            going_back = jnp.where(last_col, jnp.roll(going_back, 1, axis=1), going_back)
            returned = passed_along(going_back, "col", 1)
            matrix = matrix.at[:, :, :, tile_size - half_width :].set(updated[:, :, :, :half_width])
            matrix = matrix.at[:, :, :, :half_width].set(returned)
    return matrix.reshape(row_tiles, 1, col_tiles, 1, tile_size, tile_size)


def solution(mesh):
    placed = (P(None, "row", None, "col", None, None), P(None, None, "row", "col", None), P())
    return jax.shard_map(
        on_device,
        mesh=mesh,
        in_specs=placed,
        out_specs=P(None, "row", None, "col", None, None),
        check_vma=False,
    )
```

profile of v0, /device:TPU:39, one launch (start us, length us, event | category | flops | bytes accessed | tf_op | source)
XLA Modules:
  0.0 421.2 jit_solution(6370427126374975800)
XLA Ops:
  6.5 4.8 %copy.29 = f32[1,1,1,1,1024,1024]{5,4,3,2,1,0:T(8,128)} copy(f32[1,1,1,1,1024,1024]{5,4,3,2,1,0:T(8,128)} %param.21) | data formatting | bytes 8388608
  11.4 1.2 fusion.15
  12.6 45.0 %all_gather.3 = f32[3,1,1,512,128]{4,3,0,2,1:T(8,128)S(1)} all-gather(f32[3,1,1,32,128]{4,3,0,2,1:T(8,128)S(1)} %bitcast.123), channel_id=1, replica_groups=mesh['row'=16,'col'=16] {'col'}, dimensions={3}, use_global_device_ids=true | all-gather | bytes 835584 | tf_op jit(solution)/shard_map/all_gather | solution.py:66
  57.6 1.4 fusion.20
  59.0 4.6 %copy.6 = f32[3,128,128]{0,2,1:T(8,128)} copy(f32[3,128,128]{2,1,0:T(8,128)S(1)} %fusion.20) | data formatting | bytes 393216 | tf_op jit(solution)/shard_map/vmap()/dot_general | solution.py:40
  63.6 1.8 gather_fusion
  65.6 4.8 %copy.8 = f32[3,128,128]{0,2,1:T(8,128)} copy(f32[3,128,128]{2,1,0:T(8,128)S(1)} %select_add_fusion) | data formatting | bytes 393216 | tf_op jit(solution)/shard_map/vmap()/add | solution.py:41
  70.4 1.8 gather_fusion.1
  72.3 0.4 fusion.33
  72.7 0.4 fusion.30
  73.7 0.3 fusion.28
  74.4 0.3 fusion.26
  76.1 0.4 convolution_multiply_fusion
  76.5 0.8 fusion.18
  77.5 5.7 %select_bitcast_fusion = (f32[3,1,512,512]{3,2,0,1:T(8,128)}, f32[3,512,512]{2,1,0:T(8,128)S(1)}) fusion(f32[512,512]{1,0:T(8,128)S(1)} %copy-done.2, pred[]{:T(512)S(6)} %eq.46, pred[3]{0:T(512)(128)(4,1)S(1)} %get-tuple-element.114, f32[3,128,512]{1,2,0:T(8,128)S(1)} %fusion.18, f32[3,1,1,512,128]{4,3,0,2,1:T(8,128)} %copy-done.1), kind=kOutput, calls=%fused_computation.3 | convolution fusion | flops 1210318848 | bytes 8912900 | tf_op jit(solution)/shard_map/vmap()/dot_general | solution.py:44
  83.2 5.1 %fusion.3 = f32[512,1024]{1,0:T(8,128)S(1)} fusion(f32[1,1,1024,1024]{3,2,1,0:T(8,128)} %bitcast, f32[3,512,512]{2,1,0:T(8,128)S(1)} %get-tuple-element.120), kind=kOutput, calls=%fused_computation.12 | convolution fusion | flops 3221225472 | bytes 5242880 | tf_op jit(solution)/shard_map/ivw,ijvx->ijwx/dot_general | solution.py:93
  88.3 1.5 bitcast_dynamic-update-slice_fusion
  89.8 126.7 %all-reduce.2.cloned.1.call-done = f32[3,1,512,512]{3,2,0,1:T(8,128)} async-done(((f32[3,1,512,512]{3,2,0,1:T(8,128)}), f32[3,1,512,512]{3,2,0,1:T(8,128)}) %all-reduce.2.cloned.1.call-update) | async-done | bytes 3145744 | tf_op jit(solution)/shard_map/psum | solution.py:11
  216.5 2.8 select_select_fusion
  219.3 1.6 copy-done
  221.0 10.2 %fusion.12 = f32[1,1,1024,512]{2,3,0,1:T(8,128)} fusion(f32[1,1,1024,1024]{3,2,1,0:T(8,128)} %bitcast_dynamic-update-slice_fusion, f32[3,1,512,512]{3,2,0,1:T(8,128)S(1)} %select_select_fusion), kind=kOutput, calls=%fused_computation.24 | convolution fusion | flops 3221225472 | bytes 5242880 | tf_op jit(solution)/shard_map/ijyv,jvw->ijyw/dot_general | solution.py:96
  231.2 2.9 copy.11
  234.1 3.1 constant_dynamic-update-slice_fusion.6
  237.2 1.7 fusion.54
  239.0 16.3 %collective-permute-done = f32[1,1,256,1024]{3,2,1,0:T(8,128)S(1)} collective-permute-done((f32[1,1,256,1024]{3,2,1,0:T(8,128)S(1)}, f32[1,1,256,1024]{3,2,1,0:T(8,128)S(1)}, u32[]{:S(2)}, u32[]{:S(2)}) %collective-permute-start) | collective-permute-done | bytes 1048608 | tf_op jit(solution)/shard_map/ppermute | solution.py:17
  255.3 3.5 fusion.11
  258.8 1.5 fusion.56
  260.4 2.6 copy.12
  263.0 2.3 constant_dynamic-update-slice_fusion.5
  265.3 7.2 %collective-permute-done.1 = f32[1,1,256,1024]{2,3,1,0:T(8,128)} collective-permute-done((f32[1,1,256,1024]{2,3,1,0:T(8,128)}, f32[1,1,256,1024]{2,3,1,0:T(8,128)}, u32[]{:S(2)}, u32[]{:S(2)}) %collective-permute-start.1) | collective-permute-done | bytes 1048608 | tf_op jit(solution)/shard_map/ppermute | solution.py:17
  272.5 2.5 copy.13
  275.0 2.3 constant_dynamic-update-slice_fusion.4
  277.3 1.7 fusion.53
  279.0 5.2 %collective-permute-start.2 = (f32[1,1,1024,256]{3,2,1,0:T(8,128)S(1)}, f32[1,1,1024,256]{3,2,1,0:T(8,128)S(1)}, u32[]{:S(2)}, u32[]{:S(2)}) collective-permute-start(f32[1,1,1024,256]{3,2,1,0:T(8,128)S(1)} %get-tuple-element.116), channel_id=1, source_target_pairs={{0,15},{1,0},{2,1},{3,2},{4,3},{5,4},{6,5},{7,6},{8,7},{9,8},{10,9... | collective-permute-start | bytes 3145736 | tf_op jit(solution)/shard_map/ppermute | solution.py:17
  284.2 41.2 %collective-permute-done.2 = f32[1,1,1024,256]{3,2,1,0:T(8,128)S(1)} collective-permute-done((f32[1,1,1024,256]{3,2,1,0:T(8,128)S(1)}, f32[1,1,1024,256]{3,2,1,0:T(8,128)S(1)}, u32[]{:S(2)}, u32[]{:S(2)}) %collective-permute-start.2) | collective-permute-done | bytes 1048608 | tf_op jit(solution)/shard_map/ppermute | solution.py:17
  325.4 8.0 %fusion.10 = f32[1,1,1024,512]{2,3,0,1:T(8,128)S(1)} fusion(f32[1,1,1024,256]{3,2,1,0:T(8,128)S(1)} %collective-permute-done.2, f32[1,1,1024,256]{3,2,1,0:T(8,128)S(1)} %get-tuple-element.115, f32[3,1,512,512]{3,2,0,1:T(8,128)} %copy-done), kind=kOutput, calls=%fused_computation.22 | convolution fusion | flops 3221749760 | bytes 5242880 | tf_op jit(solution)/shard_map/ijyv,jvw->ijyw/dot_general | solution.py:115
  333.3 1.5 fusion.55
  335.0 2.6 copy.14
  337.6 2.3 constant_dynamic-update-slice_fusion.3
  339.8 46.3 %collective-permute-done.3 = f32[1,1,1024,256]{2,3,0,1:T(8,128)} collective-permute-done((f32[1,1,1024,256]{2,3,0,1:T(8,128)}, f32[1,1,1024,256]{2,3,0,1:T(8,128)}, u32[]{:S(2)}, u32[]{:S(2)}) %collective-permute-start.3) | collective-permute-done | bytes 1048608 | tf_op jit(solution)/shard_map/ppermute | solution.py:17
  386.1 2.5 copy.15
  388.7 2.3 constant_dynamic-update-slice_fusion.2
  390.9 6.4 %fusion.13 = f32[1,1,512,1024]{2,3,1,0:T(8,128)} fusion(f32[1,1,1024,1024]{3,2,1,0:T(8,128)} %constant_dynamic-update-slice_fusion.2, f32[3,512,512]{2,1,0:T(8,128)S(1)} %get-tuple-element.120), kind=kOutput, calls=%fused_computation.25 | convolution fusion | flops 3221225472 | bytes 5242880 | tf_op jit(solution)/shard_map/ivw,ijvx->ijwx/dot_general | solution.py:93
  397.3 1.9 copy.16
  399.2 1.5 constant_dynamic-update-slice_fusion.1
  400.7 10.0 %fusion.14 = f32[1,1,1,1,1024,512]{4,5,3,2,1,0:T(8,128)} fusion(f32[1,1,1024,1024]{3,2,1,0:T(8,128)} %constant_dynamic-update-slice_fusion.1, f32[3,1,512,512]{3,2,0,1:T(8,128)} %copy-done), kind=kOutput, calls=%fused_computation.26 | convolution fusion | flops 3221225472 | bytes 5242880 | tf_op jit(solution)/shard_map/ijyv,jvw->ijyw/dot_general | solution.py:96
  410.7 1.9 copy.17
  412.6 1.5 constant_dynamic-update-slice_fusion
  (30 shorter events, 3.2 us)
Async XLA Ops:
  6.5 6.0 %copy-start.3 = (f32[3,1,1,32,128]{4,3,2,1,0:T(8,128)S(1)}, f32[3,1,1,32,128]{4,3,2,1,0:T(8,128)}, u32[]{:S(2)}) copy-start(f32[3,1,1,32,128]{4,3,2,1,0:T(8,128)} %param.22) | copy-start | bytes 147460
  6.5 210.0 %all-reduce.2.cloned.1.call-start = ((), (), s32[]{:S(2)}) async-start(), calls=%async_computation | async-start | bytes 6291456 | tf_op jit(solution)/shard_map/psum | solution.py:11
  57.6 18.9 %copy-start.1 = (f32[3,1,1,512,128]{4,3,0,2,1:T(8,128)}, f32[3,1,1,512,128]{4,3,0,2,1:T(8,128)S(1)}, u32[]{:S(2)}) copy-start(f32[3,1,1,512,128]{4,3,0,2,1:T(8,128)S(1)} %all_gather.3) | copy-start | bytes 2359300
  74.1 3.2 copy-start.4
  74.1 3.4 copy-start.2
  219.3 1.6 copy-start
  238.9 16.4 %collective-permute-start = (f32[1,1,256,1024]{3,2,1,0:T(8,128)S(1)}, f32[1,1,256,1024]{3,2,1,0:T(8,128)S(1)}, u32[]{:S(2)}, u32[]{:S(2)}) collective-permute-start(f32[1,1,256,1024]{3,2,1,0:T(8,128)S(1)} %get-tuple-element.118), channel_id=1, source_target_pairs={{0,240},{16,0},{32,16},{48,32},{64,48},{80,64},{96,80},{112,96},{1... | collective-permute-start | bytes 3145736 | tf_op jit(solution)/shard_map/ppermute | solution.py:17
  260.3 12.2 %collective-permute-start.1 = (f32[1,1,256,1024]{2,3,1,0:T(8,128)}, f32[1,1,256,1024]{2,3,1,0:T(8,128)}, u32[]{:S(2)}, u32[]{:S(2)}) collective-permute-start(f32[1,1,256,1024]{2,3,1,0:T(8,128)} %get-tuple-element.123), channel_id=1, source_target_pairs={{0,16},{16,32},{32,48},{48,64},{64,80},{80,96},{96,112},{112,128},... | collective-permute-start | bytes 3145736 | tf_op jit(solution)/shard_map/ppermute | solution.py:17
  279.0 46.4 %collective-permute-start.2 = (f32[1,1,1024,256]{3,2,1,0:T(8,128)S(1)}, f32[1,1,1024,256]{3,2,1,0:T(8,128)S(1)}, u32[]{:S(2)}, u32[]{:S(2)}) collective-permute-start(f32[1,1,1024,256]{3,2,1,0:T(8,128)S(1)} %get-tuple-element.116), channel_id=1, source_target_pairs={{0,15},{1,0},{2,1},{3,2},{4,3},{5,4},{6,5},{7,6},{8,7},{9,8},{10,9... | collective-permute-start | bytes 3145736 | tf_op jit(solution)/shard_map/ppermute | solution.py:17
  334.8 51.3 %collective-permute-start.3 = (f32[1,1,1024,256]{2,3,0,1:T(8,128)}, f32[1,1,1024,256]{2,3,0,1:T(8,128)}, u32[]{:S(2)}, u32[]{:S(2)}) collective-permute-start(f32[1,1,1024,256]{2,3,0,1:T(8,128)} %get-tuple-element.121), channel_id=1, source_target_pairs={{0,1},{1,2},{2,3},{3,4},{4,5},{5,6},{6,7},{7,8},{8,9},{9,10},{10,1... | collective-permute-start | bytes 3145736 | tf_op jit(solution)/shard_map/ppermute | solution.py:17
Sparse Core Ops, SparseCore 0:
  83.3 133.1 all-reduce.1
where the time goes:
time: 425 us; the launch traced here: 421 us
  waiting for transfers between devices  238 us (56%)
  local copies, waits for them, and re-layouts  59.4 us (14%)
  matrix products  55.1 us (13%)
  blocking collectives  45 us (11%)
  between operations  14 us (3%)
  starting transfers between devices  5.63 us (1%)
  other arithmetic  4.4 us (1%)
    psum x1, waiting for transfers between devices, broadcast(): return lax.psum(kept, axis)  127 us
    ppermute x4, waiting for transfers between devices, passed_along(): return lax.ppermute(value, axis, pairs)  111 us
    all_gather x1, blocking collectives, on_device(): gathered = lax.all_gather(panels, 'col', axis=3, tiled=True)  45 us
    dot_general x2, matrix products, on_device(): jnp.einsum('ijyv,jvw->ijyw', window_cols, right_now, precision=exact_mode)  20.2 us
    dot_general x2, matrix products, on_device(): jnp.einsum('ivw,ijvx->ijwx', left_now, window_rows, precision=exact_mode)  11.5 us
  transfers between devices with their start and end apart: 5, of which 5 were waited for; matrix products, arithmetic and copies ran while one was open for 4% of the time, Pallas kernels for 0%

commit v1 on v0

v1 whole, which is shorter than its diff:
```python
import functools

import jax
import jax.numpy as jnp
from jax import lax
from jax.experimental import pallas as pl
from jax.experimental.pallas import tpu as pltpu
from jax.sharding import PartitionSpec as P

MESH = pl.DeviceIdType.MESH
F32 = jnp.float32
BF16 = jnp.bfloat16

X_N, CORE_N, Y_N, ZH_N = 4, 2, 4, 4
CHUNKS = 8
MAX_DEPTH = 4


def split(value):
    high = value.astype(BF16)
    low = (value - high.astype(F32)).astype(BF16)
    return high, low


def dot3(left, right, turned=False):
    dims = (((1,), (1 if turned else 0,)), ((), ()))

    def one(a, b):
        return lax.dot_general(a, b, dims, preferred_element_type=F32)

    return one(left[0], right[0]) + (one(left[0], right[1]) + one(left[1], right[0]))


def exact_dot(left, right):
    return jnp.dot(left, right, precision=lax.Precision.HIGHEST, preferred_element_type=F32)


def kernel(
    rows_n, cols_n, b, h_ref, panel_ref, plan_ref, out_ref,
    pack_l, pack_r, tile, high, low, pair_h, pair_l, thin_h, thin_l, turn_h, turn_l, tthin_h, tthin_l,
    f_h, f_l, ft_h, ft_l, cc_h, cc_l, u0_h, u0_l, t_own, p_own, from_below, from_above,
    st_own, sb_own, from_right, from_left, y0_h, y0_l,
    h_sem, out_sem, g_send, g_recv, y_send, y_recv, f_send, f_recv, n_send, n_recv,
    tree_send, tree_recv, up_send, up_recv, dn_send, dn_recv, rt_send, rt_recv, lf_send, lf_recv,
):
    h = b // 2
    piece = 2 * b // cols_n
    r = lax.axis_index("row")
    c = lax.axis_index("col")
    zl, x, core = r // (X_N * CORE_N), (r // CORE_N) % X_N, r % CORE_N
    y, zh = c // ZH_N, c % ZH_N

    def row_of(zl, x, core):
        return zl * (X_N * CORE_N) + x * CORE_N + core

    def col_of(y, zh):
        return y * ZH_N + zh

    active = r <= c + 1
    has_up = jnp.logical_and(active, r > 0)
    has_dn = jnp.logical_and(r < rows_n - 1, r <= c)
    has_rt = jnp.logical_and(active, c < cols_n - 1)
    has_lf = jnp.logical_and(r <= c, c > 0)

    up_dev, dn_dev = (r - 1, c), (r + 1, c)
    rt_dev, lf_dev = (r, c + 1), (r, c - 1)
    zh_dev = [(r, col_of(y, (zh + d) % ZH_N)) for d in (1, 2, 3)]
    y_up, y_dn = (y + 1) % Y_N, (y + Y_N - 1) % Y_N
    y_dev = [(r, col_of(y_up, zh)), (r, col_of(y_dn, zh))]
    core_dev = (row_of(zl, x, 1 - core), c)
    z_dev = (row_of(1 - zl, x, core), c)
    xp_dev = (row_of(zl, (x + 1) % X_N, core), c)
    xm_dev = (row_of(zl, (x + X_N - 1) % X_N, core), c)

    def remote(src, dst, send, recv, device):
        return pltpu.make_async_remote_copy(
            src_ref=src, dst_ref=dst, send_sem=send, recv_sem=recv, device_id=device, device_id_type=MESH
        )

    def tile_in(j):
        return pltpu.make_async_copy(h_ref.at[:, pl.ds(j * b, b)], tile.at[j], h_sem.at[j])

    for j in range(4):
        tile_in(j).start()

    barrier = pltpu.get_barrier_semaphore()
    around = [((r + step) % rows_n, c) for step in (1, rows_n - 1)] + [(r, (c + step) % cols_n) for step in (1, cols_n - 1)]
    peers = zh_dev + y_dev + [core_dev, z_dev, xp_dev, xm_dev] + around
    for device in peers:
        pl.semaphore_signal(barrier, inc=1, device_id=device, device_id_type=MESH)
    pl.semaphore_wait(barrier, len(peers))

    def place(k, col):
        if k == 0:
            return col * piece
        if k == 2:
            return 2 * b + col * piece
        return 4 * b + col * piece + (col // (cols_n // 2)) * (3 * b)

    def rows(k, col, skip, count):
        start = pl.multiple_of(place(k, col) + skip, 2 * piece if count > piece else piece)
        return pack_l.at[pl.ds(start, count)]

    def z_copy(d, k, col):
        return remote(panel_ref.at[k], rows(k, col, 0, piece), g_send.at[d, k], g_recv.at[d, k], zh_dev[d])

    order = (0, 2, 1)
    for k in order:
        for d in range(3):
            z_copy(d, k, c).start()
        pack_l[pl.ds(pl.multiple_of(place(k, c), piece), piece), :] = panel_ref[k]

    @pl.when(jnp.logical_not(has_dn))
    def _():
        from_below[...] = jnp.zeros_like(from_below)

    @pl.when(jnp.logical_not(has_up))
    def _():
        from_above[...] = jnp.zeros_like(from_above)
        pack_l[5 * b : 6 * b, :] = jnp.zeros((b, h), F32)
        pack_l[7 * b + h : 8 * b, :] = jnp.zeros((h, h), F32)

    @pl.when(jnp.logical_not(has_rt))
    def _():
        from_right[...] = jnp.zeros_like(from_right)

    @pl.when(jnp.logical_not(has_lf))
    def _():
        from_left[...] = jnp.zeros_like(from_left)

    def y_copy(side, k, at_y):
        block = rows(k, col_of(at_y, 0), 0, 4 * piece)
        return remote(block, block, y_send.at[side, k], y_recv.at[side, k], y_dev[side])

    def pass_copy(side, k, at_y):
        block = rows(k, col_of(at_y, 0), side * 2 * piece, 2 * piece)
        return remote(block, block, f_send.at[side, k], f_recv.at[side, k], y_dev[side])

    for k in order:
        for d in range(3):
            z_copy(d, k, col_of(y, (zh + ZH_N - 1 - d) % ZH_N)).wait_recv()
        for side in range(2):
            y_copy(side, k, y).start()
    sources = (y_dn, y_up)
    for k in order:
        for side in range(2):
            y_copy(side, k, sources[side]).wait_recv()
            pass_copy(side, k, sources[side]).start()

    for j in range(4):
        tile_in(j).wait()

    @pl.when(active)
    def _():
        @pl.loop(0, 4)
        def _(j):
            @pl.loop(0, 4)
            def _(i):
                at = pl.ds(pl.multiple_of(i * b, b), b)
                part_h, part_l = split(tile[j, at, :])
                high[j, at, :] = part_h
                low[j, at, :] = part_l

    far = (y + 2) % Y_N
    for k in order:
        for side in range(2):
            pass_copy(side, k, far).wait_recv()

    def bottom_copy():
        return remote(pack_l.at[8 * b : 9 * b], pack_l.at[5 * b : 6 * b], n_send.at[0], n_recv.at[0], dn_dev)

    def factor_copy():
        return remote(
            pack_l.at[6 * b + h : 7 * b], pack_l.at[7 * b + h : 8 * b], n_send.at[1], n_recv.at[1], dn_dev
        )

    root_zl, root_x, root_core = c // (X_N * CORE_N), (c // CORE_N) % X_N, c % CORE_N
    dx = (x + X_N - root_x) % X_N
    dz = jnp.where(zl == root_zl, 0, 1)
    dc = jnp.where(core == root_core, 0, 1)
    depth = dz + dc + jnp.where(dx == 0, 0, jnp.where(dx == 2, 2, 1))
    own = dc == 0
    is_root = r == c

    def children(q):
        even = q % 2 == 0
        odd = q % 2 == 1
        return [
            (jnp.logical_and(own, jnp.logical_or(dx == 0, jnp.logical_and(dx == 1, even))), xp_dev),
            (jnp.logical_and(own, jnp.logical_or(dx == 0, jnp.logical_and(dx == 3, odd))), xm_dev),
            (is_root, z_dev),
            (own, core_dev),
        ]

    def chunk(ref, q):
        return ref.at[pl.ds(pl.multiple_of(q * b, b), b)]

    def tree_copy(source, q, child, device):
        return remote(chunk(source, q), chunk(pack_r, q), tree_send.at[child, q], tree_recv.at[q], device)

    def hand_down(source, q):
        for child, (wanted, device) in enumerate(children(q)):

            @pl.when(wanted)
            def _():
                tree_copy(source, q, child, device).start()

    def poll(p):
        q = p - depth

        @pl.when(jnp.logical_and(depth > 0, jnp.logical_and(q >= 0, q < CHUNKS)))
        def _():
            at = jnp.clip(q, 0, CHUNKS - 1)
            tree_copy(pack_r, at, 0, core_dev).wait_recv()
            hand_down(pack_r, at)

    @pl.when(is_root)
    def _():
        @pl.loop(0, 5)
        def _(q):
            hand_down(pack_l, q)

    @pl.when(has_dn)
    def _():
        bottom_copy().start()

    def keep_f(slot, value):
        part_h, part_l = split(value)
        f_h[slot], f_l[slot] = part_h, part_l

    def keep_ft(slot, value):
        part_h, part_l = split(value.T)
        ft_h[slot], ft_l[slot] = part_h, part_l

    @pl.when(active)
    def _():
        at_row = lax.broadcasted_iota(jnp.int32, (h, h), 0)
        at_col = lax.broadcasted_iota(jnp.int32, (h, h), 1)
        eye = jnp.where(at_row == at_col, 1.0, 0.0).astype(F32)
        panels = [[pack_l[0 : 2 * b, :]], [pack_l[4 * b : 5 * b, :], pack_l[8 * b : 9 * b, :]], [pack_l[2 * b : 4 * b, :]]]
        powers, results, scales = [], [], []
        for parts in panels:
            gram = sum(exact_dot(part.T, part) for part in parts)
            upper = jnp.where(at_row < at_col, gram, jnp.where(at_row == at_col, gram * 0.5, 0.0))
            diag = jnp.where(at_row == at_col, upper, 0.0)
            power = eye - upper * (1.0 / jnp.sum(diag, axis=1, keepdims=True))
            powers.append(power)
            results.append(eye + power)
            scales.append(1.0 / jnp.sum(diag, axis=0, keepdims=True))
        span = 2
        while span < h:
            powers = [exact_dot(power, power) for power in powers]
            results = [result + exact_dot(result, power) for result, power in zip(results, powers)]
            span = span * 2
        live = [
            plan_ref[0, r] > 0,
            jnp.logical_and(plan_ref[1, r] > 0, r < rows_n - 1),
            plan_ref[2, r] > 0,
        ]
        for k in range(3):
            factor = jnp.where(live[k], results[k] * scales[k], 0.0)
            pack_l[6 * b + k * h : 6 * b + (k + 1) * h, :] = factor
            keep_ft(k, factor)

    @pl.when(has_dn)
    def _():
        factor_copy().start()

    poll(1)

    @pl.when(has_up)
    def _():
        bottom_copy().wait_recv()

    @pl.when(is_root)
    def _():
        hand_down(pack_l, 5)

    poll(2)

    def operators(pack):
        pairs = [
            jnp.concatenate([pack[0:b, :], pack[5 * b : 6 * b, :]], axis=1),
            jnp.concatenate([pack[b : 2 * b, :], pack[2 * b : 3 * b, :]], axis=1),
        ]
        thin = [pack[3 * b : 4 * b, :], pack[4 * b : 5 * b, :]]
        for at in range(2):
            pair_h[at], pair_l[at] = split(pairs[at])
            thin_h[at], thin_l[at] = split(thin[at])
        first = exact_dot(pack[5 * b : 6 * b, :].T, pack[0:b, :])
        second = exact_dot(pack[2 * b : 3 * b, :].T, pack[b : 2 * b, :])
        cc_h[...], cc_l[...] = split(jnp.concatenate([first, second], axis=0))
        return pairs, thin

    def pair(at):
        return pair_h[at], pair_l[at]

    def thinner(at):
        return thin_h[at], thin_l[at]

    def turned(at):
        return turn_h[at], turn_l[at]

    def tthin(at):
        return tthin_h[at], tthin_l[at]

    def part(col, at):
        return high[col, at, :], low[col, at, :]

    def keep(col, at, value):
        tile[col, at, :] = value
        high[col, at, :], low[col, at, :] = split(value)

    band = [slice(i * b, (i + 1) * b) for i in range(4)]

    def t_copy(j):
        return remote(t_own.at[j], from_above.at[j], dn_send.at[j], dn_recv.at[j], dn_dev)

    def p_copy(j):
        return remote(p_own.at[j], from_below.at[j], up_send.at[j], up_recv.at[j], up_dev)

    @pl.when(active)
    def _():
        pairs, thin = operators(pack_l)
        for at in range(2):
            turn_h[at], turn_l[at] = split(pairs[at].T)
            tthin_h[at], tthin_l[at] = split(thin[at].T)

    @pl.loop(0, 4)
    def _(j):
        @pl.when(active)
        def _():
            x0 = dot3(turned(0), part(j, band[0]))
            x1 = dot3(turned(1), part(j, band[1]))
            x2 = dot3(tthin(0), part(j, band[2]))
            t_own[j] = dot3(tthin(1), part(j, band[3]))
            u0 = split(dot3((ft_h[0], ft_l[0]), split(x0[:h] + x1[:h])))
            u0_h[j], u0_l[j] = u0
            shift = dot3((cc_h[...], cc_l[...]), u0)
            p_own[j] = x0[h:] - shift[:h]

            @pl.when(has_dn)
            def _():
                t_copy(j).start()

            @pl.when(has_up)
            def _():
                p_copy(j).start()

            u2 = split(dot3((ft_h[2], ft_l[2]), split(x1[h:] + x2 - shift[h:])))
            both = tuple(jnp.concatenate([a, z], axis=0) for a, z in zip(u0, u2))
            keep(j, band[1], tile[j, band[1], :] - dot3(pair(1), both))
            keep(j, band[2], tile[j, band[2], :] - dot3(thinner(0), u2))

        poll(3 + j)

    @pl.when(has_up)
    def _():
        factor_copy().wait_recv()

    @pl.when(active)
    def _():
        keep_ft(3, pack_l[7 * b + h : 8 * b, :])

    @pl.when(is_root)
    def _():
        hand_down(pack_l, 6)
        hand_down(pack_l, 7)
        pack_r[...] = pack_l[0 : 8 * b, :]

    @pl.loop(0, 4)
    def _(j):
        @pl.when(has_dn)
        def _():
            p_copy(j).wait_recv()

        @pl.when(has_up)
        def _():
            t_copy(j).wait_recv()

        @pl.when(active)
        def _():
            u1 = split(dot3((ft_h[1], ft_l[1]), split(t_own[j] + from_below[j])))
            u1p = split(dot3((ft_h[3], ft_l[3]), split(from_above[j] + p_own[j])))
            both = tuple(jnp.concatenate([a, z], axis=0) for a, z in zip((u0_h[j], u0_l[j]), u1p))
            keep(j, band[0], tile[j, band[0], :] - dot3(pair(0), both))
            keep(j, band[3], tile[j, band[3], :] - dot3(thinner(1), u1))

        poll(7 + j)

    poll(11)
    poll(12)

    def st_copy(i):
        return remote(st_own.at[i], from_left.at[i], rt_send.at[i], rt_recv.at[i], rt_dev)

    def sb_copy(i):
        return remote(sb_own.at[i], from_right.at[i], lf_send.at[i], lf_recv.at[i], lf_dev)

    def out_copy(i, j):
        at = pl.ds(pl.multiple_of(i * b, b), b)
        return pltpu.make_async_copy(tile.at[j, at], out_ref.at[at, pl.ds(j * b, b)], out_sem.at[i, j])

    @pl.when(active)
    def _():
        operators(pack_r)
        for k in range(4):
            keep_f(k, pack_r[6 * b + k * h : 6 * b + (k + 1) * h, :])

    def f_of(k):
        return f_h[k], f_l[k]

    @pl.when(active)
    def _():
        @pl.loop(0, 4)
        def _(i):
            at = pl.ds(pl.multiple_of(i * b, b), b)
            x0 = dot3(part(0, at), pair(0))
            x1 = dot3(part(1, at), pair(1))
            x2 = dot3(part(2, at), thinner(0))
            st_own[i] = dot3(part(3, at), thinner(1))
            y0 = split(dot3(split(x0[:, :h] + x1[:, :h]), f_of(0)))
            y0_h[i], y0_l[i] = y0
            shift = dot3(y0, (cc_h[...], cc_l[...]), turned=True)
            sb_own[i] = x0[:, h:] - shift[:, :h]

            @pl.when(has_rt)
            def _():
                st_copy(i).start()

            @pl.when(has_lf)
            def _():
                sb_copy(i).start()

            y2 = split(dot3(split(x1[:, h:] + x2 - shift[:, h:]), f_of(2)))
            both = tuple(jnp.concatenate([a, z], axis=1) for a, z in zip(y0, y2))
            tile[1, at, :] = tile[1, at, :] - dot3(both, pair(1), turned=True)
            tile[2, at, :] = tile[2, at, :] - dot3(y2, thinner(0), turned=True)

    @pl.loop(0, 4)
    def _(i):
        @pl.when(has_rt)
        def _():
            sb_copy(i).wait_recv()

        @pl.when(has_lf)
        def _():
            st_copy(i).wait_recv()

        @pl.when(active)
        def _():
            at = pl.ds(pl.multiple_of(i * b, b), b)
            y1 = split(dot3(split(st_own[i] + from_right[i]), f_of(1)))
            y1p = split(dot3(split(from_left[i] + sb_own[i]), f_of(3)))
            both = tuple(jnp.concatenate([a, z], axis=1) for a, z in zip((y0_h[i], y0_l[i]), y1p))
            tile[0, at, :] = tile[0, at, :] - dot3(both, pair(0), turned=True)
            tile[3, at, :] = tile[3, at, :] - dot3(y1, thinner(1), turned=True)

        for j in range(4):
            out_copy(i, j).start()

    for k in range(3):
        for d in range(3):
            z_copy(d, k, c).wait_send()
        for side in range(2):
            y_copy(side, k, y).wait_send()
            pass_copy(side, k, sources[side]).wait_send()

    @pl.when(has_dn)
    def _():
        bottom_copy().wait_send()
        factor_copy().wait_send()

    @pl.loop(0, CHUNKS)
    def _(q):
        for child, (wanted, device) in enumerate(children(q)):

            @pl.when(wanted)
            def _():
                tree_copy(pack_r, q, child, device).wait_send()

    @pl.loop(0, 4)
    def _(j):
        for there, copy in ((has_dn, t_copy), (has_up, p_copy), (has_rt, st_copy), (has_lf, sb_copy)):

            @pl.when(there)
            def _():
                copy(j).wait_send()

        for k in range(4):
            out_copy(j, k).wait()


def solution(mesh):
    rows_n, cols_n = mesh.shape["row"], mesh.shape["col"]

    def on_device(matrix_tiles, panels, plan):
        size, refl = matrix_tiles.shape[-1], panels.shape[-1]
        b, h = size // 4, refl
        piece = panels.shape[3]
        vmem, dma = pltpu.VMEM, pltpu.SemaphoreType.DMA
        scratch = [
            vmem((9 * b, h), F32), vmem((8 * b, h), F32), vmem((4, size, b), F32),
            vmem((4, size, b), BF16), vmem((4, size, b), BF16),
            vmem((2, b, b), BF16), vmem((2, b, b), BF16), vmem((2, b, h), BF16), vmem((2, b, h), BF16),
            vmem((2, b, b), BF16), vmem((2, b, b), BF16), vmem((2, h, b), BF16), vmem((2, h, b), BF16),
            vmem((4, h, h), BF16), vmem((4, h, h), BF16), vmem((4, h, h), BF16), vmem((4, h, h), BF16),
            vmem((b, h), BF16), vmem((b, h), BF16), vmem((4, h, b), BF16), vmem((4, h, b), BF16),
            vmem((4, h, b), F32), vmem((4, h, b), F32), vmem((4, h, b), F32), vmem((4, h, b), F32),
            vmem((4, b, h), F32), vmem((4, b, h), F32), vmem((4, b, h), F32), vmem((4, b, h), F32),
            vmem((4, b, h), BF16), vmem((4, b, h), BF16),
            dma((4,)), dma((4, 4)), dma((3, 3)), dma((3, 3)), dma((2, 3)), dma((2, 3)), dma((2, 3)), dma((2, 3)),
            dma((2,)), dma((2,)), dma((4, CHUNKS)), dma((CHUNKS,)),
            dma((4,)), dma((4,)), dma((4,)), dma((4,)), dma((4,)), dma((4,)), dma((4,)), dma((4,)),
        ]
        result = pl.pallas_call(
            functools.partial(kernel, rows_n, cols_n, b),
            out_shape=jax.ShapeDtypeStruct((size, size), F32),
            in_specs=[
                pl.BlockSpec(memory_space=pl.ANY),
                pl.BlockSpec(memory_space=pltpu.VMEM),
                pl.BlockSpec(memory_space=pltpu.SMEM),
            ],
            out_specs=pl.BlockSpec(memory_space=pl.ANY),
            scratch_shapes=scratch,
            compiler_params=pltpu.CompilerParams(
                collective_id=0, has_side_effects=True, vmem_limit_bytes=40 * 1024 * 1024
            ),
        )(matrix_tiles.reshape(size, size), panels.reshape(3, piece, refl), plan)
        return result.reshape(matrix_tiles.shape)

    placed = (P(None, "row", None, "col", None, None), P(None, None, "row", "col", None), P())
    return jax.shard_map(
        on_device,
        mesh=mesh,
        in_specs=placed,
        out_specs=P(None, "row", None, "col", None, None),
        check_vma=False,
    )
```

time: 425 us -> 82.6 us (0.19)
  the two profiles are of different devices: /device:TPU:39 before, /device:TPU:123 now
where the time goes in v1:
time: 82.6 us; the launch traced here: 82.3 us
  Pallas kernels  76.6 us (93%)
  local copies, waits for them, and re-layouts  5.68 us (7%)
    pallas_call x1, Pallas kernels, on_device(): pl.pallas_call(functools.partial(kernel, rows_n, cols_n, b), out_shape=ja...  76.6 us
    unnamed x7, local copies, waits for them, and re-layouts  5.68 us

profile of v1, /device:TPU:123, one launch (start us, length us, event | category | flops | bytes accessed | tf_op | source)
XLA Modules:
  0.0 82.3 jit_solution(11172052077031528208)
XLA Ops:
  0.0 0.0 copy-start
  0.0 2.2 %copy-done = f32[1,1,1,1,1024,1024]{5,4,3,2,1,0:T(8,128)S(1)} copy-done((f32[1,1,1,1,1024,1024]{5,4,3,2,1,0:T(8,128)S(1)}, f32[1,1,1,1,1024,1024]{5,4,3,2,1,0:T(8,128)}, u32[]{:S(2)}) %copy-start) | copy-done | bytes 4194328
  2.2 0.0 copy-start.1
  2.2 0.8 copy-done.1
  3.0 0.0 copy-start.2
  3.0 0.7 copy-done.2
  3.7 76.6 %shard_map.37 = f32[1024,1024]{1,0:T(8,128)S(1)} custom-call(f32[1024,1024]{1,0:T(8,128)S(1)} %bitcast.4, f32[3,32,128]{2,1,0:T(8,128)S(1)} %bitcast.5, s32[3,16]{1,0:T(4,128)S(1)} %copy-done.2), custom_call_target="tpu_custom_call" | custom-call | tf_op jit(solution)/shard_map/pallas_call | solution.py:516
  80.3 2.0 %copy.5 = f32[1,1,1,1,1024,1024]{5,4,3,2,1,0:T(8,128)} copy(f32[1,1,1,1,1024,1024]{5,4,3,2,1,0:T(8,128)S(1)} %bitcast.3) | data formatting | bytes 8388608
Async XLA Ops:
  0.0 2.2 %copy-start = (f32[1,1,1,1,1024,1024]{5,4,3,2,1,0:T(8,128)S(1)}, f32[1,1,1,1,1024,1024]{5,4,3,2,1,0:T(8,128)}, u32[]{:S(2)}) copy-start(f32[1,1,1,1,1024,1024]{5,4,3,2,1,0:T(8,128)} %param.3) | copy-start | bytes 12582916
  2.2 0.8 copy-start.1
  3.0 0.7 copy-start.2

commit v2 on v1

v2 whole, which is shorter than its diff:
```python
import functools

import jax
import jax.numpy as jnp
from jax import lax
from jax.experimental import pallas as pl
from jax.experimental.pallas import tpu as pltpu
from jax.sharding import PartitionSpec as P

MESH = pl.DeviceIdType.MESH
F32 = jnp.float32
BF16 = jnp.bfloat16

X_N, CORE_N, Y_N, ZH_N = 4, 2, 4, 4
CHUNKS = 7


def split(value):
    high = value.astype(BF16)
    low = (value - high.astype(F32)).astype(BF16)
    return high, low


def dot3(left, right, turned=False):
    side = 1 if turned else 0
    a = jnp.concatenate([left[0], left[0], left[1]], axis=1)
    z = jnp.concatenate([right[0], right[1], right[0]], axis=side)
    return lax.dot_general(a, z, (((1,), (side,)), ((), ())), preferred_element_type=F32)


def join(first, second, axis):
    return tuple(jnp.concatenate([a, z], axis=axis) for a, z in zip(first, second))


def exact_dot(left, right):
    return jnp.dot(left, right, precision=lax.Precision.HIGHEST, preferred_element_type=F32)


def kernel(
    rows_n, cols_n, b, h_ref, panel_ref, plan_hbm, out_ref,
    plan_ref, pack_l, pack_r, tile, high, low, pair_h, pair_l, thin_h, thin_l, turn_h, turn_l, tthin_h, tthin_l,
    f_h, f_l, cc_h, cc_l, t0_h, t0_l, t2_own, u2_h, u2_l, t_own, p_own, from_below, from_above,
    st_own, sb_own, from_right, from_left, y0_h, y0_l,
    in_sem, own_sem, out_sem, g_send, g_recv, y_send, y_recv, f_send, f_recv, n_send, n_recv,
    tree_send, tree_recv, row_send, row_recv, rt_send, rt_recv, lf_send, lf_recv,
):
    h = b // 2
    piece = 2 * b // cols_n
    r = lax.axis_index("row")
    c = lax.axis_index("col")
    zl, x, core = r // (X_N * CORE_N), (r // CORE_N) % X_N, r % CORE_N
    y, zh = c // ZH_N, c % ZH_N

    def row_of(zl, x, core):
        return zl * (X_N * CORE_N) + x * CORE_N + core

    def col_of(y, zh):
        return y * ZH_N + zh

    active = r <= c + 1
    has_up = jnp.logical_and(active, r > 0)
    has_dn = jnp.logical_and(r < rows_n - 1, r <= c)
    has_rt = jnp.logical_and(active, c < cols_n - 1)
    has_lf = jnp.logical_and(r <= c, c > 0)

    up_dev, dn_dev = (r - 1, c), (r + 1, c)
    rt_dev, lf_dev = (r, c + 1), (r, c - 1)
    zh_dev = [(r, col_of(y, (zh + d) % ZH_N)) for d in (1, 2, 3)]
    y_up, y_dn = (y + 1) % Y_N, (y + Y_N - 1) % Y_N
    y_dev = [(r, col_of(y_up, zh)), (r, col_of(y_dn, zh))]
    core_dev = (row_of(zl, x, 1 - core), c)
    z_dev = (row_of(1 - zl, x, core), c)
    xp_dev = (row_of(zl, (x + 1) % X_N, core), c)
    xm_dev = (row_of(zl, (x + X_N - 1) % X_N, core), c)

    def remote(src, dst, send, recv, device):
        return pltpu.make_async_remote_copy(
            src_ref=src, dst_ref=dst, send_sem=send, recv_sem=recv, device_id=device, device_id_type=MESH
        )

    tile_in = pltpu.make_async_copy(h_ref, tile, in_sem.at[0])
    plan_in = pltpu.make_async_copy(plan_hbm, plan_ref, in_sem.at[1])
    plan_in.start()
    tile_in.start()

    barrier = pltpu.get_barrier_semaphore()
    around = [((r + step) % rows_n, c) for step in (1, rows_n - 1)] + [(r, (c + step) % cols_n) for step in (1, cols_n - 1)]
    peers = zh_dev + y_dev + [core_dev, z_dev, xp_dev, xm_dev] + around
    for device in peers:
        pl.semaphore_signal(barrier, inc=1, device_id=device, device_id_type=MESH)
    pl.semaphore_wait(barrier, len(peers))

    def place(k, col):
        if k == 0:
            return col * piece
        if k == 2:
            return 2 * b + col * piece
        return 4 * b + col * piece + (col // (cols_n // 2)) * (3 * b)

    def rows(k, col, skip, count):
        start = pl.multiple_of(place(k, col) + skip, 2 * piece if count > piece else piece)
        return pack_l.at[pl.ds(start, count)]

    def z_copy(d, k, col):
        return remote(panel_ref.at[k], rows(k, col, 0, piece), g_send.at[d, k], g_recv.at[d, k], zh_dev[d])

    def own_copy(k):
        return pltpu.make_async_copy(panel_ref.at[k], rows(k, c, 0, piece), own_sem.at[k])

    order = (0, 2, 1)
    for k in order:
        for d in range(3):
            z_copy(d, k, c).start()
        own_copy(k).start()

    @pl.when(jnp.logical_not(has_dn))
    def _():
        from_below[...] = jnp.zeros_like(from_below)

    @pl.when(jnp.logical_not(has_up))
    def _():
        from_above[...] = jnp.zeros_like(from_above)
        pack_l[5 * b : 6 * b, :] = jnp.zeros((b, h), F32)
        pack_l[7 * b + h : 8 * b, :] = jnp.zeros((h, h), F32)

    @pl.when(jnp.logical_not(has_rt))
    def _():
        from_right[...] = jnp.zeros_like(from_right)

    @pl.when(jnp.logical_not(has_lf))
    def _():
        from_left[...] = jnp.zeros_like(from_left)

    root_zl, root_x, root_core = c // (X_N * CORE_N), (c // CORE_N) % X_N, c % CORE_N
    dx = (x + X_N - root_x) % X_N
    dz = jnp.where(zl == root_zl, 0, 1)
    dc = jnp.where(core == root_core, 0, 1)
    depth = dz + dc + jnp.where(dx == 0, 0, jnp.where(dx == 2, 2, 1))
    own = dc == 0
    is_root = r == c

    def children(q):
        even = q % 2 == 0
        odd = q % 2 == 1
        return [
            (jnp.logical_and(own, jnp.logical_or(dx == 0, jnp.logical_and(dx == 1, even))), xp_dev),
            (jnp.logical_and(own, jnp.logical_or(dx == 0, jnp.logical_and(dx == 3, odd))), xm_dev),
            (is_root, z_dev),
            (own, core_dev),
        ]

    def units(q):
        at_y = (y + jnp.where(q == 1, 3, jnp.where(q == 2, 1, jnp.where(q == 3, 2, 0)))) % Y_N
        panel = q < 4
        found = []
        for u, k in enumerate(order):
            start = jnp.where(panel, place(k, at_y * ZH_N), (q + 1) * b + min(u, 1) * h)
            there = jnp.logical_or(panel, u < 2) if u < 2 else jnp.logical_and(panel, at_y < Y_N // 2)
            found.append((there, pl.ds(pl.multiple_of(start, h), h)))
        return found

    def tree_copy(source, at, q, u, child, device):
        return remote(source.at[at], pack_r.at[at], tree_send.at[child, q, u], tree_recv.at[q, u], device)

    def hand_down(source, q):
        for u, (there, at) in enumerate(units(q)):
            for child, (wanted, device) in enumerate(children(q)):

                @pl.when(jnp.logical_and(wanted, there))
                def _():
                    tree_copy(source, at, q, u, child, device).start()

    def root_gives(q):
        @pl.when(is_root)
        def _():
            hand_down(pack_l, jnp.int32(q))

    def poll(p):
        q = p - depth

        @pl.when(jnp.logical_and(depth > 0, jnp.logical_and(q >= 0, q < CHUNKS)))
        def _():
            now = jnp.clip(q, 0, CHUNKS - 1)
            for u, (there, at) in enumerate(units(now)):

                @pl.when(there)
                def _():
                    tree_copy(pack_r, at, now, u, 0, core_dev).wait_recv()

            hand_down(pack_r, now)

    def y_copy(side, k, at_y):
        block = rows(k, col_of(at_y, 0), 0, 4 * piece)
        return remote(block, block, y_send.at[side, k], y_recv.at[side, k], y_dev[side])

    def pass_copy(side, k, at_y):
        block = rows(k, col_of(at_y, 0), side * 2 * piece, 2 * piece)
        return remote(block, block, f_send.at[side, k], f_recv.at[side, k], y_dev[side])

    for k in order:
        own_copy(k).wait()
        for d in range(3):
            z_copy(d, k, col_of(y, (zh + ZH_N - 1 - d) % ZH_N)).wait_recv()
        for side in range(2):
            y_copy(side, k, y).start()
    root_gives(0)

    tile_in.wait()

    @pl.when(active)
    def _():
        @pl.loop(0, 8)
        def _(i):
            at = pl.ds(pl.multiple_of(i * h, h), h)
            high[at, :], low[at, :] = split(tile[at, :])

    sources = (y_dn, y_up)
    for k in order:
        for side in range(2):
            y_copy(side, k, sources[side]).wait_recv()
            pass_copy(side, k, sources[side]).start()
    root_gives(1)
    root_gives(2)
    poll(1)
    far = (y + 2) % Y_N
    for k in order:
        for side in range(2):
            pass_copy(side, k, far).wait_recv()
    root_gives(3)

    def bottom_copy():
        return remote(pack_l.at[8 * b : 9 * b], pack_l.at[5 * b : 6 * b], n_send.at[0], n_recv.at[0], dn_dev)

    def factor_copy():
        return remote(
            pack_l.at[7 * b : 7 * b + h], pack_l.at[7 * b + h : 8 * b], n_send.at[1], n_recv.at[1], dn_dev
        )

    @pl.when(has_dn)
    def _():
        bottom_copy().start()

    poll(2)
    plan_in.wait()

    f_row = {0: 6 * b, 2: 6 * b + h, 1: 7 * b, 3: 7 * b + h}

    def keep_f(pack, slot, turned):
        value = pack[f_row[slot] : f_row[slot] + h, :]
        f_h[slot], f_l[slot] = split(value.T if turned else value)

    @pl.when(active)
    def _():
        at_row = lax.broadcasted_iota(jnp.int32, (h, h), 0)
        at_col = lax.broadcasted_iota(jnp.int32, (h, h), 1)
        eye = jnp.where(at_row == at_col, 1.0, 0.0).astype(F32)
        panels = [[pack_l[0 : 2 * b, :]], [pack_l[4 * b : 5 * b, :], pack_l[8 * b : 9 * b, :]], [pack_l[2 * b : 4 * b, :]]]
        powers, results, scales = [], [], []
        for parts in panels:
            gram = sum(exact_dot(part.T, part) for part in parts)
            upper = jnp.where(at_row < at_col, gram, jnp.where(at_row == at_col, gram * 0.5, 0.0))
            diag = jnp.where(at_row == at_col, upper, 0.0)
            power = eye - upper * (1.0 / jnp.sum(diag, axis=1, keepdims=True))
            powers.append(power)
            results.append(eye + power)
            scales.append(1.0 / jnp.sum(diag, axis=0, keepdims=True))
        span = 2
        while span < h:
            powers = [exact_dot(power, power) for power in powers]
            results = [result + exact_dot(result, power) for result, power in zip(results, powers)]
            span = span * 2
        live = [
            plan_ref[0, r] > 0,
            jnp.logical_and(plan_ref[1, r] > 0, r < rows_n - 1),
            plan_ref[2, r] > 0,
        ]
        for k in range(3):
            factor = jnp.where(live[k], results[k] * scales[k], 0.0)
            pack_l[f_row[k] : f_row[k] + h, :] = factor
            f_h[k], f_l[k] = split(factor.T)

    @pl.when(has_dn)
    def _():
        factor_copy().start()

    @pl.when(has_up)
    def _():
        bottom_copy().wait_recv()

    root_gives(4)
    root_gives(5)
    poll(3)

    def operators(pack):
        pairs = [
            jnp.concatenate([pack[0:b, :], pack[5 * b : 6 * b, :]], axis=1),
            jnp.concatenate([pack[b : 2 * b, :], pack[2 * b : 3 * b, :]], axis=1),
        ]
        thin = [pack[3 * b : 4 * b, :], pack[4 * b : 5 * b, :]]
        for at in range(2):
            pair_h[at], pair_l[at] = split(pairs[at])
            thin_h[at], thin_l[at] = split(thin[at])
        first = exact_dot(pack[5 * b : 6 * b, :].T, pack[0:b, :])
        second = exact_dot(pack[2 * b : 3 * b, :].T, pack[b : 2 * b, :])
        cc_h[...], cc_l[...] = split(jnp.concatenate([first, second], axis=0))
        return pairs, thin

    def pair(at):
        return pair_h[at], pair_l[at]

    def thinner(at):
        return thin_h[at], thin_l[at]

    def turned(at):
        return turn_h[at], turn_l[at]

    def tthin(at):
        return tthin_h[at], tthin_l[at]

    def f_of(k):
        return f_h[k], f_l[k]

    def c_of():
        return cc_h[...], cc_l[...]

    band = [slice(i * b, (i + 1) * b) for i in range(4)]

    def band_of(i):
        return high[band[i], :], low[band[i], :]

    def lower_band(i, value):
        value = tile[band[i], :] - value
        tile[band[i], :] = value
        high[band[i], :], low[band[i], :] = split(value)

    def t_copy():
        return remote(t_own, from_above, row_send.at[0], row_recv.at[0], dn_dev)

    def p_copy():
        return remote(p_own, from_below, row_send.at[1], row_recv.at[1], up_dev)

    @pl.when(active)
    def _():
        pairs, thin = operators(pack_l)
        for at in range(2):
            turn_h[at], turn_l[at] = split(pairs[at].T)
            tthin_h[at], tthin_l[at] = split(thin[at].T)
        t_own[...] = dot3(tthin(1), band_of(3))

    @pl.when(has_dn)
    def _():
        t_copy().start()

    poll(4)

    @pl.when(active)
    def _():
        x0 = dot3(turned(0), band_of(0))
        x1 = dot3(turned(1), band_of(1))
        p_own[...] = x0[h:]
        t0_h[...], t0_l[...] = split(x0[:h] + x1[:h])
        t2_own[...] = x1[h:] + dot3(tthin(0), band_of(2))
        u0 = split(dot3(f_of(0), (t0_h[...], t0_l[...])))
        t0_h[...], t0_l[...] = u0
        shift = dot3(c_of(), u0)
        p_own[...] = p_own[...] - shift[:h]
        u2_h[...], u2_l[...] = split(dot3(f_of(2), split(t2_own[...] - shift[h:])))

    @pl.when(has_up)
    def _():
        p_copy().start()
        factor_copy().wait_recv()

    root_gives(6)
    poll(5)
    poll(6)

    @pl.when(active)
    def _():
        u0, u2 = (t0_h[...], t0_l[...]), (u2_h[...], u2_l[...])
        lower_band(1, dot3(pair(1), join(u0, u2, 0)))
        lower_band(2, dot3(thinner(0), u2))
        keep_f(pack_l, 3, True)

    @pl.when(is_root)
    def _():
        pack_r[...] = pack_l[0 : 8 * b, :]

    poll(7)

    @pl.when(has_dn)
    def _():
        p_copy().wait_recv()

    @pl.when(has_up)
    def _():
        t_copy().wait_recv()

    @pl.when(active)
    def _():
        u1 = split(dot3(f_of(1), split(t_own[...] + from_below[...])))
        u1p = split(dot3(f_of(3), split(from_above[...] + p_own[...])))
        lower_band(0, dot3(pair(0), join((t0_h[...], t0_l[...]), u1p, 0)))
        lower_band(3, dot3(thinner(1), u1))

    poll(8)
    poll(9)

    def st_copy(i):
        return remote(st_own.at[i], from_left.at[i], rt_send.at[i], rt_recv.at[i], rt_dev)

    def sb_copy(i):
        return remote(sb_own.at[i], from_right.at[i], lf_send.at[i], lf_recv.at[i], lf_dev)

    def out_copy(i):
        at = pl.ds(pl.multiple_of(i * (2 * b), 2 * b), 2 * b)
        return pltpu.make_async_copy(tile.at[at], out_ref.at[at], out_sem.at[i])

    def cut(at, j):
        return high[at, band[j]], low[at, band[j]]

    @pl.when(active)
    def _():
        operators(pack_r)
        keep_f(pack_r, 0, False)
        keep_f(pack_r, 2, False)

    halves = [slice(i * 2 * b, (i + 1) * 2 * b) for i in range(2)]
    for i, at in enumerate(halves):

        @pl.when(active)
        def _():
            st_own[i] = dot3(cut(at, 3), thinner(1))
            x0 = dot3(cut(at, 0), pair(0))
            x1 = dot3(cut(at, 1), pair(1))
            y0 = split(dot3(split(x0[:, :h] + x1[:, :h]), f_of(0)))
            y0_h[i], y0_l[i] = y0
            shift = dot3(y0, c_of(), turned=True)
            sb_own[i] = x0[:, h:] - shift[:, :h]
            x2 = dot3(cut(at, 2), thinner(0))
            y2_of = split(dot3(split(x1[:, h:] + x2 - shift[:, h:]), f_of(2)))

            @pl.when(has_rt)
            def _():
                st_copy(i).start()

            @pl.when(has_lf)
            def _():
                sb_copy(i).start()

            tile[at, band[1]] = tile[at, band[1]] - dot3(join(y0, y2_of, 1), pair(1), turned=True)
            tile[at, band[2]] = tile[at, band[2]] - dot3(y2_of, thinner(0), turned=True)

    poll(10)

    @pl.when(active)
    def _():
        keep_f(pack_r, 1, False)
        keep_f(pack_r, 3, False)

    for i, at in enumerate(halves):

        @pl.when(has_rt)
        def _():
            sb_copy(i).wait_recv()

        @pl.when(has_lf)
        def _():
            st_copy(i).wait_recv()

        @pl.when(active)
        def _():
            y1 = split(dot3(split(st_own[i] + from_right[i]), f_of(1)))
            y1p = split(dot3(split(from_left[i] + sb_own[i]), f_of(3)))
            tile[at, band[0]] = tile[at, band[0]] - dot3(join((y0_h[i], y0_l[i]), y1p, 1), pair(0), turned=True)
            tile[at, band[3]] = tile[at, band[3]] - dot3(y1, thinner(1), turned=True)

        out_copy(i).start()

    for k in range(3):
        for d in range(3):
            z_copy(d, k, c).wait_send()
        for side in range(2):
            y_copy(side, k, y).wait_send()
            pass_copy(side, k, sources[side]).wait_send()

    @pl.when(has_dn)
    def _():
        bottom_copy().wait_send()
        factor_copy().wait_send()
        t_copy().wait_send()

    @pl.when(has_up)
    def _():
        p_copy().wait_send()

    @pl.loop(0, CHUNKS)
    def _(q):
        for u, (there, at) in enumerate(units(q)):
            for child, (wanted, device) in enumerate(children(q)):

                @pl.when(jnp.logical_and(wanted, there))
                def _():
                    tree_copy(pack_r, at, q, u, child, device).wait_send()

    for i in range(2):

        @pl.when(has_rt)
        def _():
            st_copy(i).wait_send()

        @pl.when(has_lf)
        def _():
            sb_copy(i).wait_send()

        out_copy(i).wait()


def solution(mesh):
    rows_n, cols_n = mesh.shape["row"], mesh.shape["col"]

    def on_device(matrix_tiles, panels, plan):
        size, refl = matrix_tiles.shape[-1], panels.shape[-1]
        b, h = size // 4, refl
        piece = panels.shape[3]
        vmem, dma = pltpu.VMEM, pltpu.SemaphoreType.DMA
        scratch = [
            pltpu.SMEM(plan.shape, jnp.int32), vmem((9 * b, h), F32), vmem((8 * b, h), F32), vmem((size, size), F32),
            vmem((size, size), BF16), vmem((size, size), BF16),
            vmem((2, b, b), BF16), vmem((2, b, b), BF16), vmem((2, b, h), BF16), vmem((2, b, h), BF16),
            vmem((2, b, b), BF16), vmem((2, b, b), BF16), vmem((2, h, b), BF16), vmem((2, h, b), BF16),
            vmem((4, h, h), BF16), vmem((4, h, h), BF16), vmem((b, h), BF16), vmem((b, h), BF16),
            vmem((h, size), BF16), vmem((h, size), BF16), vmem((h, size), F32), vmem((h, size), BF16), vmem((h, size), BF16),
            vmem((h, size), F32), vmem((h, size), F32), vmem((h, size), F32), vmem((h, size), F32),
            vmem((2, 2 * b, h), F32), vmem((2, 2 * b, h), F32), vmem((2, 2 * b, h), F32), vmem((2, 2 * b, h), F32),
            vmem((2, 2 * b, h), BF16), vmem((2, 2 * b, h), BF16),
            dma((2,)), dma((3,)), dma((2,)),
            dma((3, 3)), dma((3, 3)), dma((2, 3)), dma((2, 3)), dma((2, 3)), dma((2, 3)), dma((2,)), dma((2,)),
            dma((4, CHUNKS, 3)), dma((CHUNKS, 3)), dma((2,)), dma((2,)), dma((2,)), dma((2,)), dma((2,)), dma((2,)),
        ]
        result = pl.pallas_call(
            functools.partial(kernel, rows_n, cols_n, b),
            out_shape=jax.ShapeDtypeStruct((size, size), F32),
            in_specs=[pl.BlockSpec(memory_space=pl.ANY)] * 3,
            out_specs=pl.BlockSpec(memory_space=pl.ANY),
            scratch_shapes=scratch,
            compiler_params=pltpu.CompilerParams(
                collective_id=0, has_side_effects=True, vmem_limit_bytes=60 * 1024 * 1024
            ),
        )(matrix_tiles.reshape(size, size), panels.reshape(3, piece, refl), plan)
        return result.reshape(matrix_tiles.shape)

    placed = (P(None, "row", None, "col", None, None), P(None, None, "row", "col", None), P())
    return jax.shard_map(
        on_device,
        mesh=mesh,
        in_specs=placed,
        out_specs=P(None, "row", None, "col", None, None),
        check_vma=False,
    )
```

time: 82.6 us -> 80.2 us (0.971); the launches traced: 82.3 us -> 78.7 us
  Pallas kernels: 76.6 us -> 73.9 us
  local copies, waits for them, and re-layouts: 5.68 us -> 4.79 us
    pallas_call x1, Pallas kernels: 76.6 us -> 73.9 us  [on_device(): pl.pallas_call(functools.partial(kernel, rows_n, cols_n, b), out_shape=ja...]
    unnamed x7 -> x1, local copies, waits for them, and re-layouts: 5.68 us -> 4.79 us
where the time goes in v2:
time: 80.2 us; the launch traced here: 78.7 us
  Pallas kernels  73.9 us (92%)
  local copies, waits for them, and re-layouts  4.79 us (6%)
    pallas_call x1, Pallas kernels, on_device(): pl.pallas_call(functools.partial(kernel, rows_n, cols_n, b), out_shape=ja...  73.9 us
    unnamed x1, local copies, waits for them, and re-layouts  4.79 us

profile of v2, /device:TPU:123, one launch (start us, length us, event | category | flops | bytes accessed | tf_op | source)
XLA Modules:
  0.0 78.7 jit_solution(11989108114777363570)
XLA Ops:
  0.0 73.9 %shard_map.37 = f32[1024,1024]{1,0:T(8,128)} custom-call(f32[1024,1024]{1,0:T(8,128)} %bitcast.4, f32[3,32,128]{2,1,0:T(8,128)} %bitcast.5, s32[3,16]{1,0:T(4,128)} %plan_hbm.1), custom_call_target="tpu_custom_call" | custom-call | tf_op jit(solution)/shard_map/pallas_call | solution.py:541
  73.9 4.8 %copy.5 = f32[1,1,1,1,1024,1024]{5,4,3,2,1,0:T(8,128)} copy(f32[1,1,1,1,1024,1024]{5,4,3,2,1,0:T(8,128)} %bitcast.3) | data formatting | bytes 8388608

commit v3 on v2

v3 whole, which is shorter than its diff:
```python
import functools

import jax
import jax.numpy as jnp
from jax import lax
from jax.experimental import pallas as pl
from jax.experimental.pallas import tpu as pltpu
from jax.sharding import PartitionSpec as P

MESH = pl.DeviceIdType.MESH
F32 = jnp.float32
BF16 = jnp.bfloat16

X_N, CORE_N, Y_N, ZH_N = 4, 2, 4, 4
CHUNKS = 7


def split(value):
    high = value.astype(BF16)
    low = (value - high.astype(F32)).astype(BF16)
    return high, low


def dot3(left, right, turned=False):
    side = 1 if turned else 0
    a = jnp.concatenate([left[0], left[0], left[1]], axis=1)
    z = jnp.concatenate([right[0], right[1], right[0]], axis=side)
    return lax.dot_general(a, z, (((1,), (side,)), ((), ())), preferred_element_type=F32)


def join(first, second, axis):
    return tuple(jnp.concatenate([a, z], axis=axis) for a, z in zip(first, second))


def exact_dot(left, right):
    return jnp.dot(left, right, precision=lax.Precision.HIGHEST, preferred_element_type=F32)


def kernel(
    rows_n, cols_n, b, h_ref, panel_ref, plan_hbm, out_ref,
    plan_ref, v_l, x_l, v_r, x_r, tile, high, low, pair_h, pair_l, thin_h, thin_l, turn_h, turn_l, tthin_h, tthin_l,
    f_h, f_l, cc_h, cc_l, t0_h, t0_l, t2_own, u2_h, u2_l, t_own, p_own, from_below, from_above,
    st_own, sb_own, from_right, from_left, y0_h, y0_l, y2_own,
    in_sem, out_sem, g_send, g_recv, y_send, y_recv, f_send, f_recv, n_send, n_recv,
    tree_send, tree_recv, row_send, row_recv, rt_send, rt_recv, lf_send, lf_recv,
):
    h = b // 2
    piece = 2 * b // cols_n
    r = lax.axis_index("row")
    c = lax.axis_index("col")
    zl, x, core = r // (X_N * CORE_N), (r // CORE_N) % X_N, r % CORE_N
    y, zh = c // ZH_N, c % ZH_N

    def row_of(zl, x, core):
        return zl * (X_N * CORE_N) + x * CORE_N + core

    def col_of(y, zh):
        return y * ZH_N + zh

    active = r <= c + 1
    has_up = jnp.logical_and(active, r > 0)
    has_dn = jnp.logical_and(r < rows_n - 1, r <= c)
    has_rt = jnp.logical_and(active, c < cols_n - 1)
    has_lf = jnp.logical_and(r <= c, c > 0)

    up_dev, dn_dev = (r - 1, c), (r + 1, c)
    rt_dev, lf_dev = (r, c + 1), (r, c - 1)
    zh_dev = [(r, col_of(y, (zh + d) % ZH_N)) for d in (1, 2, 3)]
    y_up, y_dn = (y + 1) % Y_N, (y + Y_N - 1) % Y_N
    y_dev = [(r, col_of(y_up, zh)), (r, col_of(y_dn, zh))]
    core_dev = (row_of(zl, x, 1 - core), c)
    z_dev = (row_of(1 - zl, x, core), c)
    xp_dev = (row_of(zl, (x + 1) % X_N, core), c)
    xm_dev = (row_of(zl, (x + X_N - 1) % X_N, core), c)

    def remote(src, dst, send, recv, device):
        return pltpu.make_async_remote_copy(
            src_ref=src, dst_ref=dst, send_sem=send, recv_sem=recv, device_id=device, device_id_type=MESH
        )

    tile_in = pltpu.make_async_copy(h_ref, tile, in_sem.at[0])
    plan_in = pltpu.make_async_copy(plan_hbm, plan_ref, in_sem.at[1])
    plan_in.start()
    tile_in.start()

    barrier = pltpu.get_barrier_semaphore()
    around = [((r + step) % rows_n, c) for step in (1, rows_n - 1)] + [(r, (c + step) % cols_n) for step in (1, cols_n - 1)]
    peers = zh_dev + y_dev + [core_dev, z_dev, xp_dev, xm_dev] + around
    for device in peers:
        pl.semaphore_signal(barrier, inc=1, device_id=device, device_id_type=MESH)
    pl.semaphore_wait(barrier, len(peers))

    def z_copy(d, at_zh):
        at = v_l.at[y, :, pl.ds(pl.multiple_of(at_zh * piece, piece), piece)]
        return remote(panel_ref, at, g_send.at[d], g_recv.at[d], zh_dev[d])

    own_copy = pltpu.make_async_copy(panel_ref, v_l.at[y, :, pl.ds(pl.multiple_of(zh * piece, piece), piece)], in_sem.at[2])
    for d in range(3):
        z_copy(d, zh).start()
    own_copy.start()

    @pl.when(jnp.logical_not(has_dn))
    def _():
        from_below[...] = jnp.zeros_like(from_below)

    @pl.when(jnp.logical_not(has_up))
    def _():
        from_above[...] = jnp.zeros_like(from_above)
        x_l[0:2] = jnp.zeros((2, h, h), F32)
        x_l[5] = jnp.zeros((h, h), F32)

    @pl.when(jnp.logical_not(has_rt))
    def _():
        from_right[...] = jnp.zeros_like(from_right)

    @pl.when(jnp.logical_not(has_lf))
    def _():
        from_left[...] = jnp.zeros_like(from_left)

    root_zl, root_x, root_core = c // (X_N * CORE_N), (c // CORE_N) % X_N, c % CORE_N
    dx = (x + X_N - root_x) % X_N
    dz = jnp.where(zl == root_zl, 0, 1)
    dc = jnp.where(core == root_core, 0, 1)
    depth = dz + dc + jnp.where(dx == 0, 0, jnp.where(dx == 2, 2, 1))
    own = dc == 0
    is_root = r == c

    def children(q):
        even = q % 2 == 0
        odd = q % 2 == 1
        return [
            (jnp.logical_and(own, jnp.logical_or(dx == 0, jnp.logical_and(dx == 1, even))), xp_dev),
            (jnp.logical_and(own, jnp.logical_or(dx == 0, jnp.logical_and(dx == 3, odd))), xm_dev),
            (is_root, z_dev),
            (own, core_dev),
        ]

    def tree_copy(v_from, x_from, panel, q, child, device):
        send, recv = tree_send.at[child, q], tree_recv.at[q]
        if panel:
            at_y = (y + jnp.where(q == 1, 3, jnp.where(q == 2, 1, jnp.where(q == 3, 2, 0)))) % Y_N
            return remote(v_from.at[at_y], v_r.at[at_y], send, recv, device)
        at = pl.ds(2 * (q - 4), 2)
        return remote(x_from.at[at], x_r.at[at], send, recv, device)

    def hand_down(v_from, x_from, panel, q):
        for child, (wanted, device) in enumerate(children(q)):

            @pl.when(wanted)
            def _():
                tree_copy(v_from, x_from, panel, q, child, device).start()

    def root_gives(q):
        @pl.when(is_root)
        def _():
            hand_down(v_l, x_l, q < 4, jnp.int32(q))

    def poll(p):
        q = p - depth
        for panel, least, top in ((True, 0, 3), (False, 4, CHUNKS - 1)):
            if p >= least + 1:

                @pl.when(jnp.logical_and(depth > 0, jnp.logical_and(q >= least, q <= top)))
                def _():
                    now = jnp.clip(q, least, top)
                    tree_copy(v_r, x_r, panel, now, 0, core_dev).wait_recv()
                    hand_down(v_r, x_r, panel, now)

    def y_copy(side, at_y):
        block = v_l.at[at_y]
        return remote(block, block, y_send.at[side], y_recv.at[side], y_dev[side])

    def pass_copy(side, at_y):
        block = v_l.at[at_y, :, side * 2 * piece : (side + 1) * 2 * piece]
        return remote(block, block, f_send.at[side], f_recv.at[side], y_dev[side])

    own_copy.wait()
    for d in range(3):
        z_copy(d, (zh + ZH_N - 1 - d) % ZH_N).wait_recv()
    for side in range(2):
        y_copy(side, y).start()
    root_gives(0)

    tile_in.wait()

    @pl.when(active)
    def _():
        @pl.loop(0, 8)
        def _(i):
            at = pl.ds(pl.multiple_of(i * h, h), h)
            high[at, :], low[at, :] = split(tile[at, :])

    sources = (y_dn, y_up)
    for side in range(2):
        y_copy(side, sources[side]).wait_recv()
        pass_copy(side, sources[side]).start()
    root_gives(1)
    root_gives(2)
    poll(1)
    far = (y + 2) % Y_N
    for side in range(2):
        pass_copy(side, far).wait_recv()
    root_gives(3)

    def bottom_copy():
        return remote(v_l.at[2:4, 1], x_l.at[0:2], n_send.at[0], n_recv.at[0], dn_dev)

    def factor_copy():
        return remote(x_l.at[4], x_l.at[5], n_send.at[1], n_recv.at[1], dn_dev)

    @pl.when(has_dn)
    def _():
        bottom_copy().start()

    poll(2)
    plan_in.wait()

    f_at = {0: 2, 2: 3, 1: 4, 3: 5}

    @pl.when(active)
    def _():
        at_row = lax.broadcasted_iota(jnp.int32, (h, h), 0)
        at_col = lax.broadcasted_iota(jnp.int32, (h, h), 1)
        eye = jnp.where(at_row == at_col, 1.0, 0.0).astype(F32)
        powers, results, scales = [], [], []
        for k in range(3):
            panel = jnp.concatenate([v_l[at, k] for at in range(4)], axis=0)
            gram = exact_dot(panel.T, panel)
            upper = jnp.where(at_row < at_col, gram, jnp.where(at_row == at_col, gram * 0.5, 0.0))
            diag = jnp.where(at_row == at_col, upper, 0.0)
            power = eye - upper * (1.0 / jnp.sum(diag, axis=1, keepdims=True))
            powers.append(power)
            results.append(eye + power)
            scales.append(1.0 / jnp.sum(diag, axis=0, keepdims=True))
        span = 2
        while span < h:
            powers = [exact_dot(power, power) for power in powers]
            results = [result + exact_dot(result, power) for result, power in zip(results, powers)]
            span = span * 2
        live = [
            plan_ref[0, r] > 0,
            jnp.logical_and(plan_ref[1, r] > 0, r < rows_n - 1),
            plan_ref[2, r] > 0,
        ]
        for k in range(3):
            factor = jnp.where(live[k], results[k] * scales[k], 0.0)
            x_l[f_at[k]] = factor
            f_h[k], f_l[k] = split(factor.T)

    @pl.when(has_dn)
    def _():
        factor_copy().start()

    @pl.when(has_up)
    def _():
        bottom_copy().wait_recv()

    root_gives(4)
    root_gives(5)
    poll(3)

    def operators(side, v, x):
        def top(k):
            return jnp.concatenate([v[0, k], v[1, k]], axis=0)

        def bottom(k):
            return jnp.concatenate([v[2, k], v[3, k]], axis=0)

        before = jnp.concatenate([x[0], x[1]], axis=0)
        pairs = [jnp.concatenate([top(0), before], axis=1), jnp.concatenate([bottom(0), top(2)], axis=1)]
        thin = [bottom(2), top(1)]
        for at in range(2):
            pair_h[2 * side + at], pair_l[2 * side + at] = split(pairs[at])
            thin_h[2 * side + at], thin_l[2 * side + at] = split(thin[at])
        first = exact_dot(before.T, top(0))
        second = exact_dot(top(2).T, bottom(0))
        cc_h[...], cc_l[...] = split(jnp.concatenate([first, second], axis=0))
        return pairs, thin

    def pair(at):
        return pair_h[at], pair_l[at]

    def thinner(at):
        return thin_h[at], thin_l[at]

    def turned(at):
        return turn_h[at], turn_l[at]

    def tthin(at):
        return tthin_h[at], tthin_l[at]

    def f_of(k):
        return f_h[k], f_l[k]

    def c_of():
        return cc_h[...], cc_l[...]

    band = [slice(i * b, (i + 1) * b) for i in range(4)]

    def band_of(i):
        return high[band[i], :], low[band[i], :]

    def lower_band(i, value):
        value = tile[band[i], :] - value
        tile[band[i], :] = value
        high[band[i], :], low[band[i], :] = split(value)

    def t_copy():
        return remote(t_own, from_above, row_send.at[0], row_recv.at[0], dn_dev)

    def p_copy():
        return remote(p_own, from_below, row_send.at[1], row_recv.at[1], up_dev)

    @pl.when(active)
    def _():
        pairs, thin = operators(0, v_l, x_l)
        for at in range(2):
            turn_h[at], turn_l[at] = split(pairs[at].T)
            tthin_h[at], tthin_l[at] = split(thin[at].T)
        t_own[...] = dot3(tthin(1), band_of(3))

    @pl.when(has_dn)
    def _():
        t_copy().start()

    poll(4)

    @pl.when(active)
    def _():
        x0 = dot3(turned(0), band_of(0))
        x1 = dot3(turned(1), band_of(1))
        p_own[...] = x0[h:]
        t0_h[...], t0_l[...] = split(x0[:h] + x1[:h])
        t2_own[...] = x1[h:] + dot3(tthin(0), band_of(2))
        u0 = split(dot3(f_of(0), (t0_h[...], t0_l[...])))
        t0_h[...], t0_l[...] = u0
        shift = dot3(c_of(), u0)
        p_own[...] = p_own[...] - shift[:h]
        u2_h[...], u2_l[...] = split(dot3(f_of(2), split(t2_own[...] - shift[h:])))

    @pl.when(has_up)
    def _():
        p_copy().start()
        factor_copy().wait_recv()

    root_gives(6)
    poll(5)
    poll(6)

    @pl.when(active)
    def _():
        u0, u2 = (t0_h[...], t0_l[...]), (u2_h[...], u2_l[...])
        lower_band(1, dot3(pair(1), join(u0, u2, 0)))
        lower_band(2, dot3(thinner(0), u2))
        f_h[3], f_l[3] = split(x_l[5].T)

    @pl.when(is_root)
    def _():
        v_r[...] = v_l[...]
        x_r[...] = x_l[...]

    poll(7)

    poll(8)
    poll(9)

    def st_copy(i):
        return remote(st_own.at[i], from_left.at[i], rt_send.at[i], rt_recv.at[i], rt_dev)

    def sb_copy(i):
        return remote(sb_own.at[i], from_right.at[i], lf_send.at[i], lf_recv.at[i], lf_dev)

    parts = [(slice(b, 3 * b),), (slice(0, b), slice(3 * b, 4 * b))]

    def out_copies(i):
        return [
            pltpu.make_async_copy(tile.at[at], out_ref.at[at], out_sem.at[i + n]) for n, at in enumerate(parts[i])
        ]

    def cut(i, j):
        return tuple(jnp.concatenate([ref[at, band[j]] for at in parts[i]], axis=0) for ref in (high, low))

    def lower_cols(i, j, value):
        done = 0
        for at in parts[i]:
            count = at.stop - at.start
            tile[at, band[j]] = tile[at, band[j]] - value[done : done + count]
            done = done + count

    def right_start(i):
        @pl.when(active)
        def _():
            st_own[i] = dot3(cut(i, 3), thinner(3))

        @pl.when(has_rt)
        def _():
            st_copy(i).start()

        @pl.when(active)
        def _():
            x0 = dot3(cut(i, 0), pair(2))
            x1 = dot3(cut(i, 1), pair(3))
            y0 = split(dot3(split(x0[:, :h] + x1[:, :h]), f_of(4)))
            y0_h[i], y0_l[i] = y0
            shift = dot3(y0, c_of(), turned=True)
            sb_own[i] = x0[:, h:] - shift[:, :h]
            y2_own[...] = x1[:, h:] - shift[:, h:]

        @pl.when(has_lf)
        def _():
            sb_copy(i).start()

    def right_middle(i):
        @pl.when(active)
        def _():
            y2_of = split(dot3(split(y2_own[...] + dot3(cut(i, 2), thinner(2))), f_of(6)))
            lower_cols(i, 1, dot3(join((y0_h[i], y0_l[i]), y2_of, 1), pair(3), turned=True))
            lower_cols(i, 2, dot3(y2_of, thinner(2), turned=True))

    def right_end(i):
        @pl.when(has_rt)
        def _():
            sb_copy(i).wait_recv()

        @pl.when(has_lf)
        def _():
            st_copy(i).wait_recv()

        @pl.when(active)
        def _():
            y1 = split(dot3(split(st_own[i] + from_right[i]), f_of(5)))
            y1p = split(dot3(split(from_left[i] + sb_own[i]), f_of(7)))
            lower_cols(i, 0, dot3(join((y0_h[i], y0_l[i]), y1p, 1), pair(2), turned=True))
            lower_cols(i, 3, dot3(y1, thinner(3), turned=True))

        for copy in out_copies(i):
            copy.start()

    @pl.when(active)
    def _():
        operators(1, v_r, x_r)
        f_h[4], f_l[4] = split(x_r[2])
        f_h[6], f_l[6] = split(x_r[3])

    right_start(0)

    @pl.when(has_dn)
    def _():
        p_copy().wait_recv()

    @pl.when(has_up)
    def _():
        t_copy().wait_recv()

    @pl.when(active)
    def _():
        u1 = split(dot3(f_of(1), split(t_own[...] + from_below[...])))
        u1p = split(dot3(f_of(3), split(from_above[...] + p_own[...])))
        lower_band(0, dot3(pair(0), join((t0_h[...], t0_l[...]), u1p, 0)))
        lower_band(3, dot3(thinner(1), u1))

    right_middle(0)
    right_start(1)
    right_middle(1)
    poll(10)

    @pl.when(active)
    def _():
        f_h[5], f_l[5] = split(x_r[4])
        f_h[7], f_l[7] = split(x_r[5])

    right_end(0)
    right_end(1)

    for d in range(3):
        z_copy(d, zh).wait_send()
    for side in range(2):
        y_copy(side, y).wait_send()
        pass_copy(side, sources[side]).wait_send()

    @pl.when(has_dn)
    def _():
        bottom_copy().wait_send()
        factor_copy().wait_send()
        t_copy().wait_send()

    @pl.when(has_up)
    def _():
        p_copy().wait_send()

    for panel, least, top in ((True, 0, 4), (False, 4, CHUNKS)):

        @pl.loop(least, top)
        def _(q):
            for child, (wanted, device) in enumerate(children(q)):

                @pl.when(wanted)
                def _():
                    tree_copy(v_r, x_r, panel, q, child, device).wait_send()

    for i in range(2):

        @pl.when(has_rt)
        def _():
            st_copy(i).wait_send()

        @pl.when(has_lf)
        def _():
            sb_copy(i).wait_send()

        for copy in out_copies(i):
            copy.wait()


def solution(mesh):
    rows_n, cols_n = mesh.shape["row"], mesh.shape["col"]

    def on_device(matrix_tiles, panels, plan):
        size, refl = matrix_tiles.shape[-1], panels.shape[-1]
        b, h = size // 4, refl
        piece = panels.shape[3]
        vmem, dma = pltpu.VMEM, pltpu.SemaphoreType.DMA
        scratch = [
            pltpu.SMEM(plan.shape, jnp.int32),
            vmem((4, 3, h, h), F32), vmem((6, h, h), F32), vmem((4, 3, h, h), F32), vmem((6, h, h), F32),
            vmem((size, size), F32), vmem((size, size), BF16), vmem((size, size), BF16),
            vmem((4, b, b), BF16), vmem((4, b, b), BF16), vmem((4, b, h), BF16), vmem((4, b, h), BF16),
            vmem((2, b, b), BF16), vmem((2, b, b), BF16), vmem((2, h, b), BF16), vmem((2, h, b), BF16),
            vmem((8, h, h), BF16), vmem((8, h, h), BF16), vmem((b, h), BF16), vmem((b, h), BF16),
            vmem((h, size), BF16), vmem((h, size), BF16), vmem((h, size), F32), vmem((h, size), BF16), vmem((h, size), BF16),
            vmem((h, size), F32), vmem((h, size), F32), vmem((h, size), F32), vmem((h, size), F32),
            vmem((2, 2 * b, h), F32), vmem((2, 2 * b, h), F32), vmem((2, 2 * b, h), F32), vmem((2, 2 * b, h), F32),
            vmem((2, 2 * b, h), BF16), vmem((2, 2 * b, h), BF16), vmem((2 * b, h), F32),
            dma((3,)), dma((3,)),
            dma((3,)), dma((3,)), dma((2,)), dma((2,)), dma((2,)), dma((2,)), dma((2,)), dma((2,)),
            dma((4, CHUNKS)), dma((CHUNKS,)), dma((2,)), dma((2,)), dma((2,)), dma((2,)), dma((2,)), dma((2,)),
        ]
        result = pl.pallas_call(
            functools.partial(kernel, rows_n, cols_n, b),
            out_shape=jax.ShapeDtypeStruct((size, size), F32),
            in_specs=[pl.BlockSpec(memory_space=pltpu.HBM)] * 3,
            out_specs=pl.BlockSpec(memory_space=pl.ANY),
            scratch_shapes=scratch,
            compiler_params=pltpu.CompilerParams(
                collective_id=0, has_side_effects=True, vmem_limit_bytes=48 * 1024 * 1024
            ),
        )(matrix_tiles.reshape(size, size), panels.reshape(3, piece, refl), plan)
        return result.reshape(matrix_tiles.shape)

    placed = (P(None, "row", None, "col", None, None), P(None, None, "row", "col", None), P())
    return jax.shard_map(
        on_device,
        mesh=mesh,
        in_specs=placed,
        out_specs=P(None, "row", None, "col", None, None),
        check_vma=False,
    )
```

time: 80.2 us -> 77.9 us (0.971)
  the two profiles are of different devices: /device:TPU:123 before, /device:TPU:91 now
where the time goes in v3:
time: 77.9 us; the launch traced here: 77.7 us
  Pallas kernels  74.2 us (95%)
  local copies, waits for them, and re-layouts  3.49 us (4%)
    pallas_call x1, Pallas kernels, on_device(): pl.pallas_call(functools.partial(kernel, rows_n, cols_n, b), out_shape=ja...  74.2 us
    unnamed x5, local copies, waits for them, and re-layouts  3.49 us

profile of v3, /device:TPU:91, one launch (start us, length us, event | category | flops | bytes accessed | tf_op | source)
XLA Modules:
  0.0 77.7 jit_solution(1281986641558608800)
XLA Ops:
  0.0 0.0 copy-start
  0.0 0.8 %copy-done = f32[3,1,1,32,128]{4,3,2,1,0:T(8,128)S(1)} copy-done((f32[3,1,1,32,128]{4,3,2,1,0:T(8,128)S(1)}, f32[3,1,1,32,128]{4,3,2,1,0:T(8,128)}, u32[]{:S(2)}) %copy-start) | copy-done | bytes 49176
  0.8 0.0 copy-start.1
  0.8 0.7 copy-done.1
  1.5 74.2 %shard_map.37 = f32[1024,1024]{1,0:T(8,128)S(1)} custom-call(f32[1024,1024]{1,0:T(8,128)} %bitcast.5, f32[3,32,128]{2,1,0:T(8,128)S(1)} %bitcast.4, s32[3,16]{1,0:T(4,128)S(1)} %copy-done.1), custom_call_target="tpu_custom_call" | custom-call | tf_op jit(solution)/shard_map/pallas_call | solution.py:538
  75.7 2.0 %copy.5 = f32[1,1,1,1,1024,1024]{5,4,3,2,1,0:T(8,128)} copy(f32[1,1,1,1,1024,1024]{5,4,3,2,1,0:T(8,128)S(1)} %bitcast.3) | data formatting | bytes 8388608
Async XLA Ops:
  0.0 0.8 %copy-start = (f32[3,1,1,32,128]{4,3,2,1,0:T(8,128)S(1)}, f32[3,1,1,32,128]{4,3,2,1,0:T(8,128)}, u32[]{:S(2)}) copy-start(f32[3,1,1,32,128]{4,3,2,1,0:T(8,128)} %param.4) | copy-start | bytes 147460
  0.8 0.7 copy-start.1

commit v4 on v3

--- a/solution.py
+++ b/solution.py
@@ -12,7 +12,6 @@
 BF16 = jnp.bfloat16
 
 X_N, CORE_N, Y_N, ZH_N = 4, 2, 4, 4
-CHUNKS = 7
 
 
 def split(value):
@@ -42,7 +41,7 @@
     f_h, f_l, cc_h, cc_l, t0_h, t0_l, t2_own, u2_h, u2_l, t_own, p_own, from_below, from_above,
     st_own, sb_own, from_right, from_left, y0_h, y0_l, y2_own,
     in_sem, out_sem, g_send, g_recv, y_send, y_recv, f_send, f_recv, n_send, n_recv,
-    tree_send, tree_recv, row_send, row_recv, rt_send, rt_recv, lf_send, lf_recv,
+    c_send, c_recv, d_send, d_recv, k_send, k_recv, m_send, m_recv, row_send, row_recv, rt_send, rt_recv, lf_send, lf_recv,
 ):
     h = b // 2
     piece = 2 * b // cols_n
@@ -88,7 +87,25 @@
     peers = zh_dev + y_dev + [core_dev, z_dev, xp_dev, xm_dev] + around
     for device in peers:
         pl.semaphore_signal(barrier, inc=1, device_id=device, device_id_type=MESH)
-    pl.semaphore_wait(barrier, len(peers))
+    first_core = core == c % CORE_N
+    is_root = r == c
+
+    @pl.when(first_core)
+    def _():
+        @pl.loop(0, cols_n)
+        def _(col):
+            @pl.when(jnp.logical_or(r != c, col != c))
+            def _():
+                pl.semaphore_signal(barrier, inc=1, device_id=(c, col), device_id_type=MESH)
+
+            @pl.when(col >= cols_n // 2)
+            def _():
+                before = (c + rows_n - 1) % rows_n
+                pl.semaphore_signal(barrier, inc=1, device_id=(before, col), device_id_type=MESH)
+
+    chips = rows_n // CORE_N
+    expected = len(peers) + chips - jnp.where(is_root, 1, 0) + jnp.where(c >= cols_n // 2, chips, 0)
+    pl.semaphore_wait(barrier, expected)
 
     def z_copy(d, at_zh):
         at = v_l.at[y, :, pl.ds(pl.multiple_of(at_zh * piece, piece), piece)]
@@ -99,6 +116,48 @@
         z_copy(d, zh).start()
     own_copy.start()
 
+    def piece_target(n, step):
+        at_zl, at_x = (zl + n // X_N) % 2, (x + n % X_N) % X_N
+        row = row_of(at_zl, at_x, (r + step) % CORE_N)
+        return row, (row, r + step), row - row % CORE_N <= r + step + 1
+
+    def c_copy(n, col, device):
+        at_y, at_zh = col // ZH_N, col % ZH_N
+        at = v_r.at[at_y, :, pl.ds(pl.multiple_of(at_zh * piece, piece), piece)]
+        return remote(panel_ref, at, c_send.at[n], c_recv.at[col], device)
+
+    def d_copy(n, col, device):
+        at_y, at_zh = col // ZH_N - Y_N // 2, col % ZH_N
+        at = x_r.at[at_y, pl.ds(pl.multiple_of(at_zh * piece, piece), piece)]
+        return remote(panel_ref.at[1], at, d_send.at[n], d_recv.at[col - cols_n // 2], device)
+
+    self_copy = pltpu.make_async_copy(
+        panel_ref, v_r.at[y, :, pl.ds(pl.multiple_of(zh * piece, piece), piece)], in_sem.at[3]
+    )
+    gives_bottom = jnp.logical_and(c >= cols_n // 2, r < rows_n - 1)
+    served = r - core <= c + 1
+
+    def pieces_out(act):
+        for n in range(chips):
+            row, device, wanted = piece_target(n, 0)
+
+            @pl.when(jnp.logical_and(wanted, jnp.logical_or(row != r, c != r)))
+            def _():
+                act(c_copy(n, c, device))
+
+        for n in range(chips):
+            row, device, wanted = piece_target(n, 1)
+
+            @pl.when(jnp.logical_and(wanted, gives_bottom))
+            def _():
+                act(d_copy(n, jnp.maximum(c, cols_n // 2), device))
+
+    pieces_out(lambda copy: copy.start())
+
+    @pl.when(is_root)
+    def _():
+        self_copy.start()
+
     @pl.when(jnp.logical_not(has_dn))
     def _():
         from_below[...] = jnp.zeros_like(from_below)
@@ -117,54 +176,13 @@
     def _():
         from_left[...] = jnp.zeros_like(from_left)
 
-    root_zl, root_x, root_core = c // (X_N * CORE_N), (c // CORE_N) % X_N, c % CORE_N
-    dx = (x + X_N - root_x) % X_N
-    dz = jnp.where(zl == root_zl, 0, 1)
-    dc = jnp.where(core == root_core, 0, 1)
-    depth = dz + dc + jnp.where(dx == 0, 0, jnp.where(dx == 2, 2, 1))
-    own = dc == 0
-    is_root = r == c
-
-    def children(q):
-        even = q % 2 == 0
-        odd = q % 2 == 1
-        return [
-            (jnp.logical_and(own, jnp.logical_or(dx == 0, jnp.logical_and(dx == 1, even))), xp_dev),
-            (jnp.logical_and(own, jnp.logical_or(dx == 0, jnp.logical_and(dx == 3, odd))), xm_dev),
-            (is_root, z_dev),
-            (own, core_dev),
-        ]
-
-    def tree_copy(v_from, x_from, panel, q, child, device):
-        send, recv = tree_send.at[child, q], tree_recv.at[q]
-        if panel:
-            at_y = (y + jnp.where(q == 1, 3, jnp.where(q == 2, 1, jnp.where(q == 3, 2, 0)))) % Y_N
-            return remote(v_from.at[at_y], v_r.at[at_y], send, recv, device)
-        at = pl.ds(2 * (q - 4), 2)
-        return remote(x_from.at[at], x_r.at[at], send, recv, device)
-
-    def hand_down(v_from, x_from, panel, q):
-        for child, (wanted, device) in enumerate(children(q)):
-
-            @pl.when(wanted)
-            def _():
-                tree_copy(v_from, x_from, panel, q, child, device).start()
-
-    def root_gives(q):
-        @pl.when(is_root)
-        def _():
-            hand_down(v_l, x_l, q < 4, jnp.int32(q))
-
-    def poll(p):
-        q = p - depth
-        for panel, least, top in ((True, 0, 3), (False, 4, CHUNKS - 1)):
-            if p >= least + 1:
-
-                @pl.when(jnp.logical_and(depth > 0, jnp.logical_and(q >= least, q <= top)))
-                def _():
-                    now = jnp.clip(q, least, top)
-                    tree_copy(v_r, x_r, panel, now, 0, core_dev).wait_recv()
-                    hand_down(v_r, x_r, panel, now)
+    @pl.when(jnp.logical_not(has_lf))
+    def _():
+        x_r[5] = jnp.zeros((h, h), F32)
+
+    @pl.when(c == 0)
+    def _():
+        x_r[0:2] = jnp.zeros((2, h, h), F32)
 
     def y_copy(side, at_y):
         block = v_l.at[at_y]
@@ -179,7 +197,6 @@
         z_copy(d, (zh + ZH_N - 1 - d) % ZH_N).wait_recv()
     for side in range(2):
         y_copy(side, y).start()
-    root_gives(0)
 
     tile_in.wait()
 
@@ -194,13 +211,9 @@
     for side in range(2):
         y_copy(side, sources[side]).wait_recv()
         pass_copy(side, sources[side]).start()
-    root_gives(1)
-    root_gives(2)
-    poll(1)
     far = (y + 2) % Y_N
     for side in range(2):
         pass_copy(side, far).wait_recv()
-    root_gives(3)
 
     def bottom_copy():
         return remote(v_l.at[2:4, 1], x_l.at[0:2], n_send.at[0], n_recv.at[0], dn_dev)
@@ -212,19 +225,15 @@
     def _():
         bottom_copy().start()
 
-    poll(2)
     plan_in.wait()
 
-    f_at = {0: 2, 2: 3, 1: 4, 3: 5}
-
-    @pl.when(active)
-    def _():
+    def factors(v, index):
         at_row = lax.broadcasted_iota(jnp.int32, (h, h), 0)
         at_col = lax.broadcasted_iota(jnp.int32, (h, h), 1)
         eye = jnp.where(at_row == at_col, 1.0, 0.0).astype(F32)
         powers, results, scales = [], [], []
         for k in range(3):
-            panel = jnp.concatenate([v_l[at, k] for at in range(4)], axis=0)
+            panel = jnp.concatenate([v[at, k] for at in range(4)], axis=0)
             gram = exact_dot(panel.T, panel)
             upper = jnp.where(at_row < at_col, gram, jnp.where(at_row == at_col, gram * 0.5, 0.0))
             diag = jnp.where(at_row == at_col, upper, 0.0)
@@ -238,14 +247,18 @@
             results = [result + exact_dot(result, power) for result, power in zip(results, powers)]
             span = span * 2
         live = [
-            plan_ref[0, r] > 0,
-            jnp.logical_and(plan_ref[1, r] > 0, r < rows_n - 1),
-            plan_ref[2, r] > 0,
+            plan_ref[0, index] > 0,
+            jnp.logical_and(plan_ref[1, index] > 0, index < rows_n - 1),
+            plan_ref[2, index] > 0,
         ]
+        return [jnp.where(live[k], results[k] * scales[k], 0.0) for k in range(3)]
+
+    @pl.when(active)
+    def _():
+        left_factors = factors(v_l, r)
+        x_l[4] = left_factors[1]
         for k in range(3):
-            factor = jnp.where(live[k], results[k] * scales[k], 0.0)
-            x_l[f_at[k]] = factor
-            f_h[k], f_l[k] = split(factor.T)
+            f_h[k], f_l[k] = split(left_factors[k].T)
 
     @pl.when(has_dn)
     def _():
@@ -255,9 +268,40 @@
     def _():
         bottom_copy().wait_recv()
 
-    root_gives(4)
-    root_gives(5)
-    poll(3)
+    def k_copy(at):
+        return remote(v_r.at[at], v_r.at[at], k_send.at[at], k_recv.at[at], core_dev)
+
+    def l_copy():
+        return remote(x_r.at[0:2], x_r.at[0:2], k_send.at[Y_N], k_recv.at[Y_N], core_dev)
+
+    has_before = jnp.logical_and(served, c > 0)
+
+    @pl.when(jnp.logical_and(served, first_core))
+    def _():
+        @pl.loop(0, Y_N)
+        def _(at):
+            @pl.loop(0, ZH_N)
+            def _(n):
+                col = at * ZH_N + n
+
+                @pl.when(jnp.logical_or(r != c, col != c))
+                def _():
+                    c_copy(0, col, core_dev).wait_recv()
+
+                @pl.when(jnp.logical_and(r == c, col == c))
+                def _():
+                    self_copy.wait()
+
+            k_copy(at).start()
+
+    @pl.when(jnp.logical_and(has_before, first_core))
+    def _():
+        @pl.loop(cols_n // 2, cols_n)
+        def _(col):
+            d_copy(0, col, core_dev).wait_recv()
+
+        l_copy().start()
+
 
     def operators(side, v, x):
         def top(k):
@@ -323,7 +367,6 @@
     def _():
         t_copy().start()
 
-    poll(4)
 
     @pl.when(active)
     def _():
@@ -343,9 +386,6 @@
         p_copy().start()
         factor_copy().wait_recv()
 
-    root_gives(6)
-    poll(5)
-    poll(6)
 
     @pl.when(active)
     def _():
@@ -353,16 +393,6 @@
         lower_band(1, dot3(pair(1), join(u0, u2, 0)))
         lower_band(2, dot3(thinner(0), u2))
         f_h[3], f_l[3] = split(x_l[5].T)
-
-    @pl.when(is_root)
-    def _():
-        v_r[...] = v_l[...]
-        x_r[...] = x_l[...]
-
-    poll(7)
-
-    poll(8)
-    poll(9)
 
     def st_copy(i):
         return remote(st_own.at[i], from_left.at[i], rt_send.at[i], rt_recv.at[i], rt_dev)
@@ -436,11 +466,30 @@
         for copy in out_copies(i):
             copy.start()
 
+    @pl.when(jnp.logical_and(served, jnp.logical_not(first_core)))
+    def _():
+        @pl.loop(0, Y_N)
+        def _(at):
+            k_copy(at).wait_recv()
+
+    @pl.when(jnp.logical_and(has_before, jnp.logical_not(first_core)))
+    def _():
+        l_copy().wait_recv()
+
+    def m_copy():
+        return remote(x_r.at[4], x_r.at[5], m_send.at[0], m_recv.at[0], rt_dev)
+
     @pl.when(active)
     def _():
         operators(1, v_r, x_r)
-        f_h[4], f_l[4] = split(x_r[2])
-        f_h[6], f_l[6] = split(x_r[3])
+        right_factors = factors(v_r, c)
+        x_r[4] = right_factors[1]
+        for k in range(3):
+            f_h[4 + k], f_l[4 + k] = split(right_factors[k])
+
+    @pl.when(has_rt)
+    def _():
+        m_copy().start()
 
     right_start(0)
 
@@ -462,11 +511,13 @@
     right_middle(0)
     right_start(1)
     right_middle(1)
-    poll(10)
-
-    @pl.when(active)
-    def _():
-        f_h[5], f_l[5] = split(x_r[4])
+
+    @pl.when(has_lf)
+    def _():
+        m_copy().wait_recv()
+
+    @pl.when(active)
+    def _():
         f_h[7], f_l[7] = split(x_r[5])
 
     right_end(0)
@@ -488,15 +539,21 @@
     def _():
         p_copy().wait_send()
 
-    for panel, least, top in ((True, 0, 4), (False, 4, CHUNKS)):
-
-        @pl.loop(least, top)
-        def _(q):
-            for child, (wanted, device) in enumerate(children(q)):
-
-                @pl.when(wanted)
-                def _():
-                    tree_copy(v_r, x_r, panel, q, child, device).wait_send()
+    pieces_out(lambda copy: copy.wait_send())
+
+    @pl.when(jnp.logical_and(served, first_core))
+    def _():
+        @pl.loop(0, Y_N)
+        def _(at):
+            k_copy(at).wait_send()
+
+    @pl.when(jnp.logical_and(has_before, first_core))
+    def _():
+        l_copy().wait_send()
+
+    @pl.when(has_rt)
+    def _():
+        m_copy().wait_send()
 
     for i in range(2):
 
@@ -531,9 +588,9 @@
             vmem((h, size), F32), vmem((h, size), F32), vmem((h, size), F32), vmem((h, size), F32),
             vmem((2, 2 * b, h), F32), vmem((2, 2 * b, h), F32), vmem((2, 2 * b, h), F32), vmem((2, 2 * b, h), F32),
             vmem((2, 2 * b, h), BF16), vmem((2, 2 * b, h), BF16), vmem((2 * b, h), F32),
-            dma((3,)), dma((3,)),
+            dma((4,)), dma((3,)),
             dma((3,)), dma((3,)), dma((2,)), dma((2,)), dma((2,)), dma((2,)), dma((2,)), dma((2,)),
-            dma((4, CHUNKS)), dma((CHUNKS,)), dma((2,)), dma((2,)), dma((2,)), dma((2,)), dma((2,)), dma((2,)),
+            dma((8,)), dma((16,)), dma((8,)), dma((8,)), dma((5,)), dma((5,)), dma((1,)), dma((1,)), dma((2,)), dma((2,)), dma((2,)), dma((2,)), dma((2,)), dma((2,)),
         ]
         result = pl.pallas_call(
             functools.partial(kernel, rows_n, cols_n, b),

time: 77.9 us -> 73.3 us (0.941)
  the two profiles are of different devices: /device:TPU:91 before, /device:TPU:24 now
where the time goes in v4:
time: 73.3 us; the launch traced here: 73.2 us
  Pallas kernels  69.6 us (95%)
  local copies, waits for them, and re-layouts  3.49 us (5%)
    pallas_call x1, Pallas kernels, on_device(): pl.pallas_call(functools.partial(kernel, rows_n, cols_n, b), out_shape=ja...  69.6 us
    unnamed x5, local copies, waits for them, and re-layouts  3.49 us

profile of v4, /device:TPU:24, one launch (start us, length us, event | category | flops | bytes accessed | tf_op | source)
XLA Modules:
  0.0 73.2 jit_solution(18445109470607063806)
XLA Ops:
  0.0 0.0 copy-start
  0.0 0.8 %copy-done = f32[3,1,1,32,128]{4,3,2,1,0:T(8,128)S(1)} copy-done((f32[3,1,1,32,128]{4,3,2,1,0:T(8,128)S(1)}, f32[3,1,1,32,128]{4,3,2,1,0:T(8,128)}, u32[]{:S(2)}) %copy-start) | copy-done | bytes 49176
  0.8 0.0 copy-start.1
  0.8 0.7 copy-done.1
  1.5 69.6 %shard_map.37 = f32[1024,1024]{1,0:T(8,128)S(1)} custom-call(f32[1024,1024]{1,0:T(8,128)} %bitcast.5, f32[3,32,128]{2,1,0:T(8,128)S(1)} %bitcast.4, s32[3,16]{1,0:T(4,128)S(1)} %copy-done.1), custom_call_target="tpu_custom_call" | custom-call | tf_op jit(solution)/shard_map/pallas_call | solution.py:595
  71.1 2.0 %copy.5 = f32[1,1,1,1,1024,1024]{5,4,3,2,1,0:T(8,128)} copy(f32[1,1,1,1,1024,1024]{5,4,3,2,1,0:T(8,128)S(1)} %bitcast.3) | data formatting | bytes 8388608
Async XLA Ops:
  0.0 0.8 %copy-start = (f32[3,1,1,32,128]{4,3,2,1,0:T(8,128)S(1)}, f32[3,1,1,32,128]{4,3,2,1,0:T(8,128)}, u32[]{:S(2)}) copy-start(f32[3,1,1,32,128]{4,3,2,1,0:T(8,128)} %param.4) | copy-start | bytes 147460
  0.8 0.7 copy-start.1

commit v5 on v4

--- a/solution.py
+++ b/solution.py
@@ -41,7 +41,7 @@
     f_h, f_l, cc_h, cc_l, t0_h, t0_l, t2_own, u2_h, u2_l, t_own, p_own, from_below, from_above,
     st_own, sb_own, from_right, from_left, y0_h, y0_l, y2_own,
     in_sem, out_sem, g_send, g_recv, y_send, y_recv, f_send, f_recv, n_send, n_recv,
-    c_send, c_recv, d_send, d_recv, k_send, k_recv, m_send, m_recv, row_send, row_recv, rt_send, rt_recv, lf_send, lf_recv,
+    c_send, c_recv, d_send, d_recv, k_send, k_recv, m_send, m_recv, row_send, row_recv, rt_send, rt_recv, lf_send, lf_recv, pass_send,
 ):
     h = b // 2
     piece = 2 * b // cols_n
@@ -68,9 +68,22 @@
     y_up, y_dn = (y + 1) % Y_N, (y + Y_N - 1) % Y_N
     y_dev = [(r, col_of(y_up, zh)), (r, col_of(y_dn, zh))]
     core_dev = (row_of(zl, x, 1 - core), c)
-    z_dev = (row_of(1 - zl, x, core), c)
-    xp_dev = (row_of(zl, (x + 1) % X_N, core), c)
-    xm_dev = (row_of(zl, (x + X_N - 1) % X_N, core), c)
+
+    def relay_col(col):
+        return col_of(Y_N - 1 - col // ZH_N, col % ZH_N)
+
+    def relayed(col):
+        low_rows = jnp.logical_and(r >= rows_n // 2, r > relay_col(col) + 1)
+        return jnp.logical_and(low_rows, col // ZH_N >= Y_N // 2)
+
+    rt_relay = jnp.logical_and(zh < ZH_N - 1, relayed(c))
+    lf_relay = jnp.logical_and(zh > 0, relayed(c))
+    rt_first = (r, jnp.where(rt_relay, relay_col(c), c + 1))
+    lf_first = (r, jnp.where(lf_relay, relay_col(c), c - 1))
+    served_col = relay_col(c)
+    is_relay = jnp.logical_and(y < Y_N // 2, relayed(served_col))
+    pass_rt = jnp.logical_and(is_relay, jnp.logical_and(zh < ZH_N - 1, r <= served_col + 1))
+    pass_lf = jnp.logical_and(is_relay, jnp.logical_and(zh > 0, r <= served_col))
 
     def remote(src, dst, send, recv, device):
         return pltpu.make_async_remote_copy(
@@ -84,7 +97,9 @@
 
     barrier = pltpu.get_barrier_semaphore()
     around = [((r + step) % rows_n, c) for step in (1, rows_n - 1)] + [(r, (c + step) % cols_n) for step in (1, cols_n - 1)]
-    peers = zh_dev + y_dev + [core_dev, z_dev, xp_dev, xm_dev] + around
+    mirror = Y_N - 1 - y
+    relay_peers = [(r, col_of(mirror, (zh + step) % ZH_N)) for step in (1, ZH_N - 1)]
+    peers = zh_dev + y_dev + [core_dev] + around + relay_peers
     for device in peers:
         pl.semaphore_signal(barrier, inc=1, device_id=device, device_id_type=MESH)
     first_core = core == c % CORE_N
@@ -158,25 +173,25 @@
     def _():
         self_copy.start()
 
-    @pl.when(jnp.logical_not(has_dn))
+    @pl.when(jnp.logical_and(active, jnp.logical_not(has_dn)))
     def _():
         from_below[...] = jnp.zeros_like(from_below)
 
-    @pl.when(jnp.logical_not(has_up))
+    @pl.when(jnp.logical_and(active, jnp.logical_not(has_up)))
     def _():
         from_above[...] = jnp.zeros_like(from_above)
         x_l[0:2] = jnp.zeros((2, h, h), F32)
         x_l[5] = jnp.zeros((h, h), F32)
 
-    @pl.when(jnp.logical_not(has_rt))
+    @pl.when(jnp.logical_and(active, jnp.logical_not(has_rt)))
     def _():
         from_right[...] = jnp.zeros_like(from_right)
 
-    @pl.when(jnp.logical_not(has_lf))
+    @pl.when(jnp.logical_and(active, jnp.logical_not(has_lf)))
     def _():
         from_left[...] = jnp.zeros_like(from_left)
 
-    @pl.when(jnp.logical_not(has_lf))
+    @pl.when(jnp.logical_and(active, jnp.logical_not(has_lf)))
     def _():
         x_r[5] = jnp.zeros((h, h), F32)
 
@@ -268,41 +283,6 @@
     def _():
         bottom_copy().wait_recv()
 
-    def k_copy(at):
-        return remote(v_r.at[at], v_r.at[at], k_send.at[at], k_recv.at[at], core_dev)
-
-    def l_copy():
-        return remote(x_r.at[0:2], x_r.at[0:2], k_send.at[Y_N], k_recv.at[Y_N], core_dev)
-
-    has_before = jnp.logical_and(served, c > 0)
-
-    @pl.when(jnp.logical_and(served, first_core))
-    def _():
-        @pl.loop(0, Y_N)
-        def _(at):
-            @pl.loop(0, ZH_N)
-            def _(n):
-                col = at * ZH_N + n
-
-                @pl.when(jnp.logical_or(r != c, col != c))
-                def _():
-                    c_copy(0, col, core_dev).wait_recv()
-
-                @pl.when(jnp.logical_and(r == c, col == c))
-                def _():
-                    self_copy.wait()
-
-            k_copy(at).start()
-
-    @pl.when(jnp.logical_and(has_before, first_core))
-    def _():
-        @pl.loop(cols_n // 2, cols_n)
-        def _(col):
-            d_copy(0, col, core_dev).wait_recv()
-
-        l_copy().start()
-
-
     def operators(side, v, x):
         def top(k):
             return jnp.concatenate([v[0, k], v[1, k]], axis=0)
@@ -384,6 +364,44 @@
     @pl.when(has_up)
     def _():
         p_copy().start()
+
+    def k_copy(at):
+        return remote(v_r.at[at], v_r.at[at], k_send.at[at], k_recv.at[at], core_dev)
+
+    def l_copy():
+        return remote(x_r.at[0:2], x_r.at[0:2], k_send.at[Y_N], k_recv.at[Y_N], core_dev)
+
+    has_before = jnp.logical_and(served, c > 0)
+
+    @pl.when(jnp.logical_and(served, first_core))
+    def _():
+        @pl.loop(0, Y_N)
+        def _(at):
+            @pl.loop(0, ZH_N)
+            def _(n):
+                col = at * ZH_N + n
+
+                @pl.when(jnp.logical_or(r != c, col != c))
+                def _():
+                    c_copy(0, col, core_dev).wait_recv()
+
+                @pl.when(jnp.logical_and(r == c, col == c))
+                def _():
+                    self_copy.wait()
+
+            k_copy(at).start()
+
+    @pl.when(jnp.logical_and(has_before, first_core))
+    def _():
+        @pl.loop(cols_n // 2, cols_n)
+        def _(col):
+            d_copy(0, col, core_dev).wait_recv()
+
+        l_copy().start()
+
+
+    @pl.when(has_up)
+    def _():
         factor_copy().wait_recv()
 
 
@@ -395,10 +413,10 @@
         f_h[3], f_l[3] = split(x_l[5].T)
 
     def st_copy(i):
-        return remote(st_own.at[i], from_left.at[i], rt_send.at[i], rt_recv.at[i], rt_dev)
+        return remote(st_own.at[i], from_left.at[i], rt_send.at[i], rt_recv.at[i], rt_dev if i else rt_first)
 
     def sb_copy(i):
-        return remote(sb_own.at[i], from_right.at[i], lf_send.at[i], lf_recv.at[i], lf_dev)
+        return remote(sb_own.at[i], from_right.at[i], lf_send.at[i], lf_recv.at[i], lf_dev if i else lf_first)
 
     parts = [(slice(b, 3 * b),), (slice(0, b), slice(3 * b, 4 * b))]
 
@@ -417,15 +435,16 @@
             tile[at, band[j]] = tile[at, band[j]] - value[done : done + count]
             done = done + count
 
+    def right_first(i):
+        @pl.when(active)
+        def _():
+            st_own[i] = dot3(cut(i, 3), thinner(3))
+
+        @pl.when(has_rt)
+        def _():
+            st_copy(i).start()
+
     def right_start(i):
-        @pl.when(active)
-        def _():
-            st_own[i] = dot3(cut(i, 3), thinner(3))
-
-        @pl.when(has_rt)
-        def _():
-            st_copy(i).start()
-
         @pl.when(active)
         def _():
             x0 = dot3(cut(i, 0), pair(2))
@@ -482,16 +501,33 @@
     @pl.when(active)
     def _():
         operators(1, v_r, x_r)
+
+    right_first(0)
+
+    @pl.when(active)
+    def _():
         right_factors = factors(v_r, c)
         x_r[4] = right_factors[1]
         for k in range(3):
             f_h[4 + k], f_l[4 + k] = split(right_factors[k])
 
+    relay_copies = [
+        (pass_rt, st_copy, remote(from_left.at[0], from_left.at[0], pass_send.at[0], rt_recv.at[0], (r, served_col + 1))),
+        (pass_lf, sb_copy, remote(from_right.at[0], from_right.at[0], pass_send.at[1], lf_recv.at[0], (r, served_col - 1))),
+    ]
+    for there, arrived, onward in relay_copies:
+
+        @pl.when(there)
+        def _():
+            arrived(0).wait_recv()
+            onward.start()
+
+    right_start(0)
+
     @pl.when(has_rt)
     def _():
         m_copy().start()
 
-    right_start(0)
 
     @pl.when(has_dn)
     def _():
@@ -509,6 +545,7 @@
         lower_band(3, dot3(thinner(1), u1))
 
     right_middle(0)
+    right_first(1)
     right_start(1)
     right_middle(1)
 
@@ -540,6 +577,11 @@
         p_copy().wait_send()
 
     pieces_out(lambda copy: copy.wait_send())
+    for there, _, onward in relay_copies:
+
+        @pl.when(there)
+        def _():
+            onward.wait_send()
 
     @pl.when(jnp.logical_and(served, first_core))
     def _():
@@ -590,7 +632,7 @@
             vmem((2, 2 * b, h), BF16), vmem((2, 2 * b, h), BF16), vmem((2 * b, h), F32),
             dma((4,)), dma((3,)),
             dma((3,)), dma((3,)), dma((2,)), dma((2,)), dma((2,)), dma((2,)), dma((2,)), dma((2,)),
-            dma((8,)), dma((16,)), dma((8,)), dma((8,)), dma((5,)), dma((5,)), dma((1,)), dma((1,)), dma((2,)), dma((2,)), dma((2,)), dma((2,)), dma((2,)), dma((2,)),
+            dma((8,)), dma((16,)), dma((8,)), dma((8,)), dma((5,)), dma((5,)), dma((1,)), dma((1,)), dma((2,)), dma((2,)), dma((2,)), dma((2,)), dma((2,)), dma((2,)), dma((2,)),
         ]
         result = pl.pallas_call(
             functools.partial(kernel, rows_n, cols_n, b),

time: 73.3 us -> 71.5 us (0.975)
  the two profiles are of different devices: /device:TPU:24 before, /device:TPU:123 now
where the time goes in v5:
time: 71.5 us; the launch traced here: 71.3 us
  Pallas kernels  67.8 us (95%)
  local copies, waits for them, and re-layouts  3.49 us (5%)
    pallas_call x1, Pallas kernels, on_device(): pl.pallas_call(functools.partial(kernel, rows_n, cols_n, b), out_shape=ja...  67.8 us
    unnamed x5, local copies, waits for them, and re-layouts  3.49 us

profile of v5, /device:TPU:123, one launch (start us, length us, event | category | flops | bytes accessed | tf_op | source)
XLA Modules:
  0.0 71.3 jit_solution(15574132262911916131)
XLA Ops:
  0.0 0.0 copy-start
  0.0 0.8 %copy-done = f32[3,1,1,32,128]{4,3,2,1,0:T(8,128)S(1)} copy-done((f32[3,1,1,32,128]{4,3,2,1,0:T(8,128)S(1)}, f32[3,1,1,32,128]{4,3,2,1,0:T(8,128)}, u32[]{:S(2)}) %copy-start) | copy-done | bytes 49176
  0.8 0.0 copy-start.1
  0.8 0.7 copy-done.1
  1.5 67.8 %shard_map.37 = f32[1024,1024]{1,0:T(8,128)S(1)} custom-call(f32[1024,1024]{1,0:T(8,128)} %bitcast.5, f32[3,32,128]{2,1,0:T(8,128)S(1)} %bitcast.4, s32[3,16]{1,0:T(4,128)S(1)} %copy-done.1), custom_call_target="tpu_custom_call" | custom-call | tf_op jit(solution)/shard_map/pallas_call | solution.py:637
  69.3 2.0 %copy.5 = f32[1,1,1,1,1024,1024]{5,4,3,2,1,0:T(8,128)} copy(f32[1,1,1,1,1024,1024]{5,4,3,2,1,0:T(8,128)S(1)} %bitcast.3) | data formatting | bytes 8388608
Async XLA Ops:
  0.0 0.8 %copy-start = (f32[3,1,1,32,128]{4,3,2,1,0:T(8,128)S(1)}, f32[3,1,1,32,128]{4,3,2,1,0:T(8,128)}, u32[]{:S(2)}) copy-start(f32[3,1,1,32,128]{4,3,2,1,0:T(8,128)} %param.4) | copy-start | bytes 147460
  0.8 0.7 copy-start.1

commit v6 on v5

--- a/solution.py
+++ b/solution.py
@@ -242,12 +242,12 @@
 
     plan_in.wait()
 
-    def factors(v, index):
+    def factors(v, index, chosen):
         at_row = lax.broadcasted_iota(jnp.int32, (h, h), 0)
         at_col = lax.broadcasted_iota(jnp.int32, (h, h), 1)
         eye = jnp.where(at_row == at_col, 1.0, 0.0).astype(F32)
         powers, results, scales = [], [], []
-        for k in range(3):
+        for k in chosen:
             panel = jnp.concatenate([v[at, k] for at in range(4)], axis=0)
             gram = exact_dot(panel.T, panel)
             upper = jnp.where(at_row < at_col, gram, jnp.where(at_row == at_col, gram * 0.5, 0.0))
@@ -266,11 +266,11 @@
             jnp.logical_and(plan_ref[1, index] > 0, index < rows_n - 1),
             plan_ref[2, index] > 0,
         ]
-        return [jnp.where(live[k], results[k] * scales[k], 0.0) for k in range(3)]
-
-    @pl.when(active)
-    def _():
-        left_factors = factors(v_l, r)
+        return [jnp.where(live[k], results[n] * scales[n], 0.0) for n, k in enumerate(chosen)]
+
+    @pl.when(active)
+    def _():
+        left_factors = factors(v_l, r, (0, 1, 2))
         x_l[4] = left_factors[1]
         for k in range(3):
             f_h[k], f_l[k] = split(left_factors[k].T)
@@ -506,10 +506,7 @@
 
     @pl.when(active)
     def _():
-        right_factors = factors(v_r, c)
-        x_r[4] = right_factors[1]
-        for k in range(3):
-            f_h[4 + k], f_l[4 + k] = split(right_factors[k])
+        f_h[4], f_l[4] = split(factors(v_r, c, (0,))[0])
 
     relay_copies = [
         (pass_rt, st_copy, remote(from_left.at[0], from_left.at[0], pass_send.at[0], rt_recv.at[0], (r, served_col + 1))),
@@ -523,6 +520,13 @@
             onward.start()
 
     right_start(0)
+
+    @pl.when(active)
+    def _():
+        second, third = factors(v_r, c, (1, 2))
+        x_r[4] = second
+        f_h[5], f_l[5] = split(second)
+        f_h[6], f_l[6] = split(third)
 
     @pl.when(has_rt)
     def _():

time: 71.5 us -> 70.6 us (0.987)
  Pallas kernels: 67.8 us -> 66.9 us
    pallas_call x1, Pallas kernels: 67.8 us -> 66.9 us  [on_device(): pl.pallas_call(functools.partial(kernel, rows_n, cols_n, b), out_shape=ja...]
where the time goes in v6:
time: 70.6 us; the launch traced here: 70.4 us
  Pallas kernels  66.9 us (95%)
  local copies, waits for them, and re-layouts  3.49 us (5%)
    pallas_call x1, Pallas kernels, on_device(): pl.pallas_call(functools.partial(kernel, rows_n, cols_n, b), out_shape=ja...  66.9 us
    unnamed x5, local copies, waits for them, and re-layouts  3.49 us

profile of v6, /device:TPU:123, one launch (start us, length us, event | category | flops | bytes accessed | tf_op | source)
XLA Modules:
  0.0 70.4 jit_solution(9277857753841548875)
XLA Ops:
  0.0 0.0 copy-start
  0.0 0.8 %copy-done = f32[3,1,1,32,128]{4,3,2,1,0:T(8,128)S(1)} copy-done((f32[3,1,1,32,128]{4,3,2,1,0:T(8,128)S(1)}, f32[3,1,1,32,128]{4,3,2,1,0:T(8,128)}, u32[]{:S(2)}) %copy-start) | copy-done | bytes 49176
  0.8 0.0 copy-start.1
  0.8 0.7 copy-done.1
  1.5 66.9 %shard_map.37 = f32[1024,1024]{1,0:T(8,128)S(1)} custom-call(f32[1024,1024]{1,0:T(8,128)} %bitcast.5, f32[3,32,128]{2,1,0:T(8,128)S(1)} %bitcast.4, s32[3,16]{1,0:T(4,128)S(1)} %copy-done.1), custom_call_target="tpu_custom_call" | custom-call | tf_op jit(solution)/shard_map/pallas_call | solution.py:641
  68.4 2.0 %copy.5 = f32[1,1,1,1,1024,1024]{5,4,3,2,1,0:T(8,128)} copy(f32[1,1,1,1,1024,1024]{5,4,3,2,1,0:T(8,128)S(1)} %bitcast.3) | data formatting | bytes 8388608
Async XLA Ops:
  0.0 0.8 %copy-start = (f32[3,1,1,32,128]{4,3,2,1,0:T(8,128)S(1)}, f32[3,1,1,32,128]{4,3,2,1,0:T(8,128)}, u32[]{:S(2)}) copy-start(f32[3,1,1,32,128]{4,3,2,1,0:T(8,128)} %param.4) | copy-start | bytes 147460
  0.8 0.7 copy-start.1
